TPU v7x, 256 devices: a whole 4x4x8 slice. The times are simulated.
256 devices in a mesh: pat: 4 (over z_lo), vox: 64 (over z_hi, x, y, core).
Axes of the slice: x: 4, y: 4, z: 8 (z_hi: 2, z_lo: 4; z = z_hi * 4 + z_lo), core: 2. Of those that a mesh axis runs over, the one named last changes fastest.
Arguments:
- conductivity: float32 [128, 128, 128], P('vox'), may hold values from 0.3 to 1.5
- warm_forward: float32 [128, 32, 128, 128], P('vox', 'pat'), may hold values from -3 to 3
- warm_adjoint: float32 [128, 32, 128, 128], P('vox', 'pat'), may hold values from -3 to 3
- electrodes: int32 [128], replicated, may hold values from 0 to 2097151
- patterns: int32 [32, 4], P('pat'), may hold values from 0 to 127, all different within a row
- observed: float32 [32], P('pat'), may hold values from -16 to 16
Outputs:
- gradient: float32 [128, 128, 128], P('vox')
- predicted: float32 [32], P('pat')
All inputs are finite; a program needn't handle non-finite values.
Results may differ from a plain program's by a relative error of at most 0.0003.
Values sent between devices are 32-bit elements; how exact they have to be, the bound alone decides.
A program may use at most 64 MiB of HBM per device.

v0:
```python
import math

import jax
import jax.numpy as jnp
from jax import lax
from jax.sharding import PartitionSpec as P

ITERS = 2


leakage = 0.05


def extended(block, sides, width):
    for axis, dim in sides:
        count = lax.axis_size(axis)
        forward = [(i, i + 1) for i in range(count - 1)]
        backward = [(target, source) for source, target in forward]
        low = lax.ppermute(
            lax.slice_in_dim(block, block.shape[dim] - width, None, axis=dim), axis, forward
        )
        high = lax.ppermute(lax.slice_in_dim(block, 0, width, axis=dim), axis, backward)
        block = jnp.concatenate([low, block, high], axis=dim)
    return block


def both_sides(values, along_axis):
    lower_pad = [(0, 0)] * values.ndim
    upper_pad = [(0, 0)] * values.ndim
    lower_pad[along_axis] = (1, 0)
    upper_pad[along_axis] = (0, 1)
    return jnp.pad(values, lower_pad) + jnp.pad(values, upper_pad)


def spread(values, along_axis):
    lower_pad = [(0, 0)] * values.ndim
    upper_pad = [(0, 0)] * values.ndim
    lower_pad[along_axis] = (1, 0)
    upper_pad[along_axis] = (0, 1)
    return jnp.pad(values, lower_pad) - jnp.pad(values, upper_pad)


def operate(values, coeffs):
    depth_faces, row_faces, column_faces = coeffs
    padded = extended(values, (("vox", 0),), 1)
    flux_depth = depth_faces[:, None] * (padded[1:] - padded[:-1])
    result = leakage * values + (flux_depth[:-1] - flux_depth[1:])
    result = result + spread(row_faces[:, None] * (values[:, :, 1:] - values[:, :, :-1]), 2)
    result = result + spread(
        column_faces[:, None] * (values[:, :, :, 1:] - values[:, :, :, :-1]), 3
    )
    return result


def inner(left_factor, right_factor):
    return jnp.sum(left_factor * right_factor, axis=(0, 2, 3))


def widen(vector):
    return vector[None, :, None, None]


def pattern_sum(local_terms):
    return lax.psum(local_terms, "vox")


def solve_pattern(right_side, initial, coeffs, diagonal):
    solution = initial
    residue = right_side - operate(solution, coeffs)
    precond = residue / diagonal
    direction = precond
    current = pattern_sum(inner(residue, precond))
    for iteration in range(ITERS):
        applied = operate(direction, coeffs)
        step_size = current / pattern_sum(inner(direction, applied))
        solution = solution + widen(step_size) * direction
        residue = residue - widen(step_size) * applied
        if iteration + 1 < ITERS:
            precond = residue / diagonal
            following = pattern_sum(inner(residue, precond))
            direction = precond + widen(following / current) * direction
            current = following
    return solution


def per_device(conductivity, warm_forward, warm_adjoint, electrodes, patterns, observed):
    plane_count, pattern_count, row_count, column_count = warm_forward.shape
    position = lax.axis_index("vox")
    layers = lax.axis_size("vox")
    strength = 2.0 * math.sqrt(layers * plane_count * row_count * column_count)
    data_weight = 0.1 * strength
    lower_open = (position > 0).astype(jnp.float32)
    upper_open = (position < layers - 1).astype(jnp.float32)
    padded_sigma = extended(conductivity, (("vox", 0),), 1)
    face_mask = jnp.concatenate(
        [lower_open[None], jnp.ones((plane_count - 1,), jnp.float32), upper_open[None]]
    )
    depth_faces = 0.5 * (padded_sigma[1:] + padded_sigma[:-1]) * face_mask[:, None, None]
    row_faces = 0.5 * (conductivity[:, 1:] + conductivity[:, :-1])
    column_faces = 0.5 * (conductivity[:, :, 1:] + conductivity[:, :, :-1])
    coeffs = (depth_faces, row_faces, column_faces)
    diagonal = (
        leakage
        + (depth_faces[:-1] + depth_faces[1:])
        + both_sides(row_faces, 1)
        + both_sides(column_faces, 2)
    )
    diagonal = diagonal[:, None]
    electrode_ids = jnp.arange(electrodes.shape[0], dtype=jnp.int32)
    picked = jnp.sum(
        jnp.where(
            patterns[:, :, None] == electrode_ids[None, None, :], electrodes[None, None, :], 0
        ),
        axis=2,
    )
    offset = position * (plane_count * row_count * column_count)
    local_cell = picked - offset
    grid_shape = (plane_count, 1, row_count, column_count)
    cell_index = (
        lax.broadcasted_iota(jnp.int32, grid_shape, 0) * row_count
        + lax.broadcasted_iota(jnp.int32, grid_shape, 2)
    ) * column_count + lax.broadcasted_iota(jnp.int32, grid_shape, 3)

    def marker(which_one):
        return (cell_index == local_cell[:, which_one][None, :, None, None]).astype(jnp.float32)

    forward = solve_pattern(strength * (marker(0) - marker(1)), warm_forward, coeffs, diagonal)
    probe_weights = marker(2) - marker(3)
    predicted = lax.psum(inner(probe_weights, forward), "vox")
    misfit = predicted - observed
    adjoint = solve_pattern(
        widen(data_weight * misfit) * probe_weights, warm_adjoint, coeffs, diagonal
    )
    stacked = jnp.concatenate([forward, adjoint], axis=1)
    padded_pair = extended(stacked, (("vox", 0),), 1)
    padded_forward = padded_pair[:, :pattern_count]
    padded_adjoint = padded_pair[:, pattern_count:]
    depth_products = jnp.sum(
        (padded_forward[1:] - padded_forward[:-1]) * (padded_adjoint[1:] - padded_adjoint[:-1]),
        axis=1,
    )
    depth_products = depth_products * face_mask[:, None, None]
    grad_depth = depth_products[:-1] + depth_products[1:]
    row_products = jnp.sum(
        (forward[:, :, 1:] - forward[:, :, :-1]) * (adjoint[:, :, 1:] - adjoint[:, :, :-1]), axis=1
    )
    column_products = jnp.sum(
        (forward[:, :, :, 1:] - forward[:, :, :, :-1])
        * (adjoint[:, :, :, 1:] - adjoint[:, :, :, :-1]),
        axis=1,
    )
    local_gradient = -0.5 * (
        grad_depth + both_sides(row_products, 1) + both_sides(column_products, 2)
    )
    gradient = lax.psum(local_gradient, "pat")
    return (gradient, predicted)


def solution(mesh):
    in_specs = (
        P("vox", None, None),
        P("vox", "pat", None, None),
        P("vox", "pat", None, None),
        P(),
        P("pat", None),
        P("pat"),
    )
    out_specs = (P("vox", None, None), P("pat"))
    return jax.shard_map(
        per_device, mesh=mesh, in_specs=in_specs, out_specs=out_specs, check_vma=False
    )
```

profile of v0, /device:TPU:8, one launch (start us, length us, event | category | flops | bytes accessed | tf_op | source)
XLA Modules:
  0.0 1665.2 jit_solution(10204874562504707592)
XLA Ops:
  7.2 1.0 fusion.63
  8.2 1.9 collective-permute-start
  10.1 2.4 collective-permute-start.1
  12.5 2.1 fusion.61
  14.6 3.8 collective-permute-start.2
  18.5 1.9 collective-permute-start.3
  20.4 1.1 fusion.62
  21.5 3.0 collective-permute-start.9
  24.7 0.7 iota_add_fusion
  25.7 0.3 subtract_multiply_fusion.2
  26.5 2.5 collective-permute-done.3
  29.1 1.3 fusion.2
  30.4 0.8 broadcast_divide_fusion.1
  31.4 2.1 collective-permute-start.4
  33.4 2.5 collective-permute-start.5
  36.0 0.3 fusion.36
  36.5 3.6 collective-permute-done.4
  40.1 4.0 collective-permute-done.5
  44.3 1.7 multiply_reduce_fusion.5
  46.0 196.2 %all-reduce.33 = (f32[8]{0:T(128)S(1)}, f32[8]{0:T(128)S(1)}) all-reduce(f32[8]{0:T(128)S(1)} %get-tuple-element.5, f32[8]{0:T(128)S(1)} %get-tuple-element.4), channel_id=1, replica_groups=mesh['pat'=4,'vox'=64] {'vox'}, use_global_device_ids=true, to_apply=%region_2.3 | all-reduce | flops 16 | bytes 128 | tf_op jit(solution)/shard_map/psum | solution.py:64
  242.2 1.6 multiply_reduce_fusion.4
  243.8 9.4 collective-permute-start.8
  253.2 193.9 %psum.72 = f32[8]{0:T(128)S(1)} all-reduce(f32[8]{0:T(128)S(1)} %multiply_reduce_fusion.4), channel_id=1, replica_groups=mesh['pat'=4,'vox'=64] {'vox'}, use_global_device_ids=true, to_apply=%region_6.7 | all-reduce | flops 8 | bytes 64 | tf_op jit(solution)/shard_map/psum | solution.py:64
  447.1 1.8 multiply_add_fusion.3
  449.1 10.6 collective-permute-start.6
  459.8 2.1 collective-permute-start.7
  461.8 1.6 fusion.29
  463.4 1.3 fusion.30
  464.7 1.7 collective-permute-done.6
  466.4 4.0 collective-permute-done.7
  470.4 2.8 fusion.4
  473.2 0.7 fusion.35
  473.9 190.2 %psum.73 = f32[8]{0:T(128)S(1)} all-reduce(f32[8]{0:T(128)S(1)} %fusion.35), channel_id=1, replica_groups=mesh['pat'=4,'vox'=64] {'vox'}, use_global_device_ids=true, to_apply=%region_8.9 | all-reduce | flops 8 | bytes 64 | tf_op jit(solution)/shard_map/psum | solution.py:64
  664.1 2.8 multiply_reduce_fusion.3
  666.9 200.9 %psum.74 = f32[8]{0:T(128)S(1)} all-reduce(f32[8]{0:T(128)S(1)} %get-tuple-element.15), channel_id=1, replica_groups=mesh['pat'=4,'vox'=64] {'vox'}, use_global_device_ids=true, to_apply=%region_10.11 | all-reduce | flops 8 | bytes 64 | tf_op jit(solution)/shard_map/psum | solution.py:129
  867.9 3.7 broadcast_divide_fusion
  871.7 11.8 collective-permute-start.10
  883.5 2.1 collective-permute-start.11
  885.6 0.3 fusion.20
  886.1 4.1 collective-permute-done.10
  890.2 4.0 collective-permute-done.11
  894.4 0.8 multiply_reduce_fusion.1
  895.2 190.2 %all-reduce.32 = (f32[8]{0:T(128)S(1)}, f32[8]{0:T(128)S(1)}) all-reduce(f32[8]{0:T(128)S(1)} %get-tuple-element.3, f32[8]{0:T(128)S(1)} %get-tuple-element.2), channel_id=1, replica_groups=mesh['pat'=4,'vox'=64] {'vox'}, use_global_device_ids=true, to_apply=%region_12.13 | all-reduce | flops 16 | bytes 128 | tf_op jit(solution)/shard_map/psum | solution.py:64
  1085.4 0.3 multiply_reduce_fusion
  1085.8 201.1 %psum.77 = f32[8]{0:T(128)S(1)} all-reduce(f32[8]{0:T(128)S(1)} %multiply_reduce_fusion), channel_id=1, replica_groups=mesh['pat'=4,'vox'=64] {'vox'}, use_global_device_ids=true, to_apply=%region_16.17 | all-reduce | flops 8 | bytes 64 | tf_op jit(solution)/shard_map/psum | solution.py:64
  1286.9 1.5 multiply_add_fusion.1
  1288.5 11.8 collective-permute-start.12
  1300.3 2.1 collective-permute-start.13
  1302.3 0.3 fusion.13
  1302.9 4.1 collective-permute-done.12
  1306.9 4.0 collective-permute-done.13
  1311.1 0.7 fusion.19
  1311.8 190.2 %psum.78 = f32[8]{0:T(128)S(1)} all-reduce(f32[8]{0:T(128)S(1)} %fusion.19), channel_id=1, replica_groups=mesh['pat'=4,'vox'=64] {'vox'}, use_global_device_ids=true, to_apply=%region_18.19 | all-reduce | flops 8 | bytes 64 | tf_op jit(solution)/shard_map/psum | solution.py:64
  1502.3 0.9 copy-done.2
  1503.5 6.9 collective-permute-start.14
  1510.4 1.9 collective-permute-start.15
  1512.3 0.6 fusion.10
  1513.2 9.5 collective-permute-done.14
  1522.6 7.6 collective-permute-done.15
  1530.3 0.8 pad_maximum_fusion
  1531.1 0.6 fusion.1
  1531.8 0.8 fusion.48
  1532.6 124.2 %all-reduce.36.cloned.1.call-done = f32[2,128,128]{2,1,0:T(8,128)} async-done(((f32[2,128,128]{2,1,0:T(8,128)}), f32[2,128,128]{2,1,0:T(8,128)}) %all-reduce.36.cloned.1.call-update) | async-done | bytes 131088 | tf_op jit(solution)/shard_map/psum | solution.py:155
  1656.8 1.6 copy.10
  (80 shorter events, 3.1 us)
Async XLA Ops:
  7.2 13.2 copy-start
  7.2 1649.6 %all-reduce.36.cloned.1.call-start = ((), (), s32[]{:S(2)}) async-start(), calls=%async_computation | async-start | bytes 262144 | tf_op jit(solution)/shard_map/psum | solution.py:155
  8.2 18.1 %collective-permute-start = (f32[1,128,128]{2,1,0:T(8,128)S(1)}, f32[1,128,128]{2,1,0:T(8,128)S(1)}, u32[]{:S(2)}, u32[]{:S(2)}) collective-permute-start(f32[1,128,128]{2,1,0:T(8,128)S(1)} %get-tuple-element.43), channel_id=1, source_target_pairs={{1,0},{2,1},{3,2},{4,3},{5,4},{6,5},{7,6},{8,7},{9,8},{10,9},{11,1... | collective-permute-start | bytes 196616 | tf_op jit(solution)/shard_map/ppermute | solution.py:22
  10.1 16.2 collective-permute-start.1
  14.6 9.9 copy-start.15
  14.6 10.8 copy-start.17
  14.6 10.8 copy-start.18
  14.6 11.1 copy-start.1
  14.6 11.9 collective-permute-start.2
  18.5 10.6 collective-permute-start.3
  21.5 443.2 %collective-permute-start.9 = (f32[1,8,128,128]{3,2,1,0:T(8,128)}, f32[1,8,128,128]{3,2,1,0:T(8,128)}, u32[]{:S(2)}, u32[]{:S(2)}) collective-permute-start(f32[1,8,128,128]{3,2,1,0:T(8,128)} %get-tuple-element.34), channel_id=1, source_target_pairs={{0,1},{1,2},{2,3},{3,4},{4,5},{5,6},{6,7},{7,8},{8,9},{9,10},{10,1... | collective-permute-start | bytes 1572872 | tf_op jit(solution)/shard_map/ppermute | solution.py:19
  24.6 1.7 copy-start.10
  24.7 1.7 copy-start.5
  26.5 3.9 copy-start.16
  31.3 210.9 %copy-start.3 = (f32[2,8,128,128]{3,2,1,0:T(8,128)}, f32[2,8,128,128]{3,2,1,0:T(8,128)S(1)}, u32[]{:S(2)}) copy-start(f32[2,8,128,128]{3,2,1,0:T(8,128)S(1)} %get-tuple-element.19) | copy-start | bytes 3145732
  31.3 4.7 copy-start.11
  31.4 8.7 collective-permute-start.4
  33.4 2.9 copy-start.6
  33.4 10.6 collective-permute-start.5
  243.8 220.9 %collective-permute-start.8 = (f32[1,8,128,128]{3,2,1,0:T(8,128)}, f32[1,8,128,128]{3,2,1,0:T(8,128)}, u32[]{:S(2)}, u32[]{:S(2)}) collective-permute-start(f32[1,8,128,128]{3,2,1,0:T(8,128)} %get-tuple-element.35), channel_id=1, source_target_pairs={{1,0},{2,1},{3,2},{4,3},{5,4},{6,5},{7,6},{8,7},{9,8},{10,9},{11,1... | collective-permute-start | bytes 1572872 | tf_op jit(solution)/shard_map/ppermute | solution.py:22
  449.0 12.8 copy-start.12
  449.1 17.3 %collective-permute-start.6 = (f32[1,8,128,128]{3,2,1,0:T(8,128)S(1)}, f32[1,8,128,128]{3,2,1,0:T(8,128)S(1)}, u32[]{:S(2)}, u32[]{:S(2)}) collective-permute-start(f32[1,8,128,128]{3,2,1,0:T(8,128)S(1)} %get-tuple-element.29), channel_id=1, source_target_pairs={{1,0},{2,1},{3,2},{4,3},{5,4},{6,5},{7,6},{8,7},{9,8},{10,9},{11,1... | collective-permute-start | bytes 1572872 | tf_op jit(solution)/shard_map/ppermute | solution.py:22
  459.7 3.7 copy-start.7
  459.8 10.7 collective-permute-start.7
  664.1 203.8 %copy-start.19 = (f32[8]{0:T(128)S(1)}, f32[8]{0:T(128)}, u32[]{:S(2)}) copy-start(f32[8]{0:T(128)} %param.11) | copy-start | bytes 100
  867.9 3.8 copy-start.20
  871.6 13.9 copy-start.13
  871.7 18.5 %collective-permute-start.10 = (f32[1,8,128,128]{3,2,1,0:T(8,128)S(1)}, f32[1,8,128,128]{3,2,1,0:T(8,128)S(1)}, u32[]{:S(2)}, u32[]{:S(2)}) collective-permute-start(f32[1,8,128,128]{3,2,1,0:T(8,128)S(1)} %get-tuple-element.27), channel_id=1, source_target_pairs={{1,0},{2,1},{3,2},{4,3},{5,4},{6,5},{7,6},{8,7},{9,8},{10,9},{11,1... | collective-permute-start | bytes 1572872 | tf_op jit(solution)/shard_map/ppermute | solution.py:22
  883.5 2.4 copy-start.8
  883.5 10.6 collective-permute-start.11
  895.2 391.7 %copy-start.4 = (f32[2,8,128,128]{3,2,1,0:T(8,128)}, f32[2,8,128,128]{3,2,1,0:T(8,128)S(1)}, u32[]{:S(2)}) copy-start(f32[2,8,128,128]{3,2,1,0:T(8,128)S(1)} %get-tuple-element.12) | copy-start | bytes 3145732
  1288.4 13.9 copy-start.14
  1288.5 18.5 %collective-permute-start.12 = (f32[1,8,128,128]{3,2,1,0:T(8,128)S(1)}, f32[1,8,128,128]{3,2,1,0:T(8,128)S(1)}, u32[]{:S(2)}, u32[]{:S(2)}) collective-permute-start(f32[1,8,128,128]{3,2,1,0:T(8,128)S(1)} %get-tuple-element.25), channel_id=1, source_target_pairs={{1,0},{2,1},{3,2},{4,3},{5,4},{6,5},{7,6},{8,7},{9,8},{10,9},{11,1... | collective-permute-start | bytes 1572872 | tf_op jit(solution)/shard_map/ppermute | solution.py:22
  1300.3 2.4 copy-start.9
  1300.3 10.6 collective-permute-start.13
  1502.0 1.2 copy-start.2
  1503.5 19.2 %collective-permute-start.14 = (f32[1,16,128,128]{3,2,1,0:T(8,128)S(1)}, f32[1,16,128,128]{3,2,1,0:T(8,128)S(1)}, u32[]{:S(2)}, u32[]{:S(2)}) collective-permute-start(f32[1,16,128,128]{3,2,1,0:T(8,128)S(1)} %get-tuple-element.22), channel_id=1, source_target_pairs={{1,0},{2,1},{3,2},{4,3},{5,4},{6,5},{7,6},{8,7},{9,8},{10,9},{11,1... | collective-permute-start | bytes 3145736 | tf_op jit(solution)/shard_map/ppermute | solution.py:22
  1510.4 19.9 %collective-permute-start.15 = (f32[1,16,128,128]{3,2,1,0:T(8,128)S(1)}, f32[1,16,128,128]{3,2,1,0:T(8,128)S(1)}, u32[]{:S(2)}, u32[]{:S(2)}) collective-permute-start(f32[1,16,128,128]{3,2,1,0:T(8,128)S(1)} %get-tuple-element.23), channel_id=1, source_target_pairs={{0,1},{1,2},{2,3},{3,4},{4,5},{5,6},{6,7},{7,8},{8,9},{9,10},{10,1... | collective-permute-start | bytes 3145736 | tf_op jit(solution)/shard_map/ppermute | solution.py:19
Sparse Core Ops, SparseCore 0:
  1532.7 123.9 all-reduce.35
where the time goes:
time: 1670 us
  blocking collectives  1360 us (81%)
  waiting for transfers between devices  173 us (10%)
  starting transfers between devices  76.3 us (5%)
  other arithmetic  31.2 us (2%)
    psum x6, blocking collectives, pattern_sum(): return lax.psum(local_terms, 'vox')  1160 us
    psum x1, blocking collectives, per_device(): predicted = lax.psum(inner(probe_weights, forward), 'vox')  201 us
    psum x1, waiting for transfers between devices, per_device(): gradient = lax.psum(local_gradient, 'pat')  124 us
    ppermute x8, starting transfers between devices, extended(): lax.ppermute(lax.slice_in_dim(block, 0, width, axis=dim), axis, backward)  58.3 us
  transfers between devices with their start and end apart: 17, of which 12 were waited for; matrix products, arithmetic and copies ran while one was open for 1% of the time, Pallas kernels for 0%

commit v1 on v0

v1 whole, which is shorter than its diff:
```python
import functools
import math

import jax
import jax.numpy as jnp
from jax import lax
from jax.experimental import pallas as pl
from jax.experimental.pallas import tpu as pltpu
from jax.sharding import PartitionSpec as P

MESH = pl.DeviceIdType.MESH
LEAK = 0.05
N = 128
PLANE = N * N
PC = 8

ZL, ZH, XM, XP, YM, YP, DG, DI = range(8)


def up_row(x):
    return pltpu.roll(x, N - 1, 0)


def down_row(x):
    return pltpu.roll(x, 1, 0)


def up_col(x):
    return pltpu.roll(x, N - 1, 1)


def down_col(x):
    return pltpu.roll(x, 1, 1)


def total(x):
    part = jnp.sum(x.reshape(N // 8, 8, N), axis=0)
    return jnp.sum(jnp.sum(part, axis=1, keepdims=True), axis=0, keepdims=True)


def kernel(
    npat,
    layers,
    group,
    strength,
    cond,
    wf,
    wa,
    elec,
    pats,
    obs,
    grad_out,
    pred_out,
    sh,
    xh,
    dh,
    wh,
    d0,
    w0,
    dc,
    co,
    dih,
    acc,
    tile,
    red,
    kc,
    gb,
    rsb,
    agb,
    sig_s,
    sig_r,
    hs,
    hr,
    red_s,
    red_r,
    rs_s,
    rs_r,
    ag_s,
    ag_r,
):
    q = lax.axis_index("pat")
    v = lax.axis_index("vox")
    has_lo = v > 0
    has_hi = v < layers - 1
    groups = layers // group
    rank = (lax.rem(v, group), v // group)
    sizes = (group, groups)
    warm = (wf, wa)
    data_weight = 0.1 * strength
    chunk = N // npat

    def member(stage, k):
        return (v // group) * group + k if stage == 0 else k * group + lax.rem(v, group)

    barrier = pltpu.get_barrier_semaphore()

    def greet(device):
        pl.semaphore_signal(barrier, inc=1, device_id=device, device_id_type=MESH)

    @pl.when(has_lo)
    def _():
        greet((q, v - 1))

    @pl.when(has_hi)
    def _():
        greet((q, v + 1))

    for stage in range(2):
        for j in range(1, sizes[stage]):
            greet((q, member(stage, lax.rem(rank[stage] + j, sizes[stage]))))
    for j in range(1, npat):
        greet((lax.rem(q + j, npat), v))

    rows = lax.broadcasted_iota(jnp.int32, (N, N), 0)
    cols = lax.broadcasted_iota(jnp.int32, (N, N), 1)
    cell = rows * N + cols
    trow = lax.broadcasted_iota(jnp.int32, (PC, N), 0)
    tcol = lax.broadcasted_iota(jnp.int32, (PC, N), 1)

    @pl.when(jnp.logical_not(has_lo))
    def _():
        sh[0] = jnp.zeros((2, N, N), jnp.float32)

        @pl.loop(0, PC)
        def _(p):
            for s in range(2):
                for h in (xh, dh, wh):
                    h[s, 0, p] = jnp.zeros((N, N), jnp.float32)

    @pl.when(jnp.logical_not(has_hi))
    def _():
        sh[1] = jnp.zeros((2, N, N), jnp.float32)

        @pl.loop(0, PC)
        def _(p):
            for s in range(2):
                for h in (xh, dh, wh):
                    h[s, 1, p] = jnp.zeros((N, N), jnp.float32)

    tile[...] = jnp.zeros((2, PC, N), jnp.float32)
    acc[...] = jnp.zeros((7, N, N), jnp.float32)

    partners = (sizes[0] - 1) + (sizes[1] - 1) + (npat - 1)
    pl.semaphore_wait(
        barrier, partners + has_lo.astype(jnp.int32) + has_hi.astype(jnp.int32)
    )

    def sig_copy(d):
        return pltpu.make_async_remote_copy(
            cond, sh.at[d], sig_s.at[d], sig_r.at[d],
            device_id=(q, v + 1 - 2 * d), device_id_type=MESH,
        )

    def halo_copy(stage, s, d, p):
        plane = 1 - d
        if stage == 0:
            src, dst = warm[s].at[plane, p], xh.at[s, d, p]
        elif stage == 1:
            src, dst = d0.at[s, p, plane], dh.at[s, d, p]
        else:
            src, dst = w0.at[s, p, plane], wh.at[s, d, p]
        return pltpu.make_async_remote_copy(
            src, dst, hs.at[stage, s, d, p], hr.at[stage, s, d, p],
            device_id=(q, v + 1 - 2 * d), device_id_type=MESH,
        )

    def send_halo(stage, s, p):
        @pl.when(has_hi)
        def _():
            halo_copy(stage, s, 0, p).start()

        @pl.when(has_lo)
        def _():
            halo_copy(stage, s, 1, p).start()

    def await_halo(stage, s, p):
        @pl.when(has_lo)
        def _():
            halo_copy(stage, s, 0, p).wait_recv()

        @pl.when(has_hi)
        def _():
            halo_copy(stage, s, 1, p).wait_recv()

    @pl.when(has_hi)
    def _():
        sig_copy(0).start()

    @pl.when(has_lo)
    def _():
        sig_copy(1).start()

    @pl.loop(0, PC)
    def _(p):
        send_halo(0, 0, p)

    @pl.when(has_lo)
    def _():
        sig_copy(0).wait_recv()

    @pl.when(has_hi)
    def _():
        sig_copy(1).wait_recv()

    lo_open = has_lo.astype(jnp.float32)
    hi_open = has_hi.astype(jnp.float32)
    s0, s1 = cond[0], cond[1]
    slo, shi = sh[0, 1], sh[1, 0]
    z_lo = 0.5 * (s0 + slo) * lo_open
    z_mid = 0.5 * (s0 + s1)
    z_hi = 0.5 * (s1 + shi) * hi_open

    def in_plane(s):
        xp = jnp.where(rows < N - 1, 0.5 * (s + up_row(s)), 0.0)
        yp = jnp.where(cols < N - 1, 0.5 * (s + up_col(s)), 0.0)
        return xp, down_row(xp), yp, down_col(yp)

    for plane, (s, below, above) in enumerate(((s0, z_lo, z_mid), (s1, z_mid, z_hi))):
        xp, xm, yp, ym = in_plane(s)
        diag = LEAK + (below + above) + (xp + xm) + (yp + ym)
        inv = 1.0 / diag
        for k, value in ((ZL, below), (ZH, above), (XM, xm), (XP, xp), (YM, ym), (YP, yp)):
            co[k, plane] = value * inv
        co[DG, plane] = diag
        co[DI, plane] = inv
    for d, (s, near, far) in enumerate(((slo, z_lo, sh[0, 0]), (shi, z_hi, sh[1, 1]))):
        xp, xm, yp, ym = in_plane(s)
        dih[d] = 1.0 / (LEAK + (near + 0.5 * (s + far)) + (xp + xm) + (yp + ym))

    def apply(a, b, lo, hi):
        out = []
        for plane, (x, below, above) in enumerate(((a, lo, b), (b, a, hi))):
            y = co[ZL, plane] * below + co[ZH, plane] * above
            y = y + co[XM, plane] * down_row(x) + co[XP, plane] * up_row(x)
            y = y + co[YM, plane] * down_col(x) + co[YP, plane] * up_col(x)
            out.append(x - y)
        return out

    def voxel(p, which):
        return elec[pats[p, which]]

    def difference(p, first, second, plane, scale):
        here = (2 * v + plane) * PLANE
        plus = jnp.where(cell == voxel(p, first) - here, scale, 0.0)
        return plus - jnp.where(cell == voxel(p, second) - here, scale, 0.0)

    def record(r, p, values):
        now = tile[r]
        for k, value in values:
            now = jnp.where((trow == p) & (tcol == k), value, now)
        tile[r] = now

    def first(s):
        @pl.loop(0, PC)
        def _(p):
            await_halo(0, s, p)
            a, b = warm[s][0, p], warm[s][1, p]
            y0, y1 = apply(a, b, xh[s, 0, p], xh[s, 1, p])
            if s == 0:
                e0 = difference(p, 0, 1, 0, strength) * co[DI, 0] - y0
                e1 = difference(p, 0, 1, 1, strength) * co[DI, 1] - y1
            else:
                e0, e1 = -y0, -y1
            d0[s, p, 0] = e0
            d0[s, p, 1] = e1
            send_halo(1, s, p)
            if s == 0:
                send_halo(0, 1, p)
                g0 = difference(p, 2, 3, 0, 1.0)
                g1 = difference(p, 2, 3, 1, 1.0)
                record(0, p, (
                    (0, total(co[DG, 0] * e0 * e0 + co[DG, 1] * e1 * e1)),
                    (4, total(g0 * a + g1 * b)),
                    (5, total(g0 * e0 + g1 * e1)),
                ))

    def second(s):
        @pl.loop(0, PC)
        def _(p):
            await_halo(1, s, p)
            a, b, lo, hi = d0[s, p, 0], d0[s, p, 1], dh[s, 0, p], dh[s, 1, p]
            if s == 1:
                weight = kc[2, pl.ds(p, 1), :]
                a = a + weight * (difference(p, 2, 3, 0, 1.0) * co[DI, 0])
                b = b + weight * (difference(p, 2, 3, 1, 1.0) * co[DI, 1])
                lo = lo + weight * (difference(p, 2, 3, -1, 1.0) * dih[0])
                hi = hi + weight * (difference(p, 2, 3, 2, 1.0) * dih[1])
                dc[p, 0] = a
                dc[p, 1] = b
                dh[s, 0, p] = lo
                dh[s, 1, p] = hi
            y0, y1 = apply(a, b, lo, hi)
            w0[s, p, 0] = y0
            w0[s, p, 1] = y1
            send_halo(2, s, p)
            u0, u1 = co[DG, 0] * y0, co[DG, 1] * y1
            values = [(1, total(u0 * a + u1 * b)), (2, total(u0 * y0 + u1 * y1))]
            if s == 0:
                g0 = difference(p, 2, 3, 0, 1.0)
                g1 = difference(p, 2, 3, 1, 1.0)
                values.append((6, total(g0 * y0 + g1 * y1)))
            else:
                values.append((0, total(co[DG, 0] * a * a + co[DG, 1] * b * b)))
            record(s, p, values)

    def third(s):
        @pl.loop(0, PC)
        def _(p):
            await_halo(2, s, p)
            a, b = w0[s, p, 0], w0[s, p, 1]
            y0, y1 = apply(a, b, wh[s, 0, p], wh[s, 1, p])
            record(s, p, ((3, total(co[DG, 0] * a * y0 + co[DG, 1] * b * y1)),))

    def sum_copy(r, stage, k, slot):
        return pltpu.make_async_remote_copy(
            red.at[r, stage, slot], red.at[r, stage, slot],
            red_s.at[r, stage, k], red_r.at[r, stage, slot],
            device_id=(q, member(stage, k)), device_id_type=MESH,
        )

    def sum_over_vox(r):
        value = tile[r]
        for stage in range(2):
            mine, size = rank[stage], sizes[stage]
            red[r, stage, mine] = value
            for j in range(1, size):
                sum_copy(r, stage, lax.rem(mine + j, size), mine).start()
            for j in range(1, size):
                k = lax.rem(mine + j, size)
                sum_copy(r, stage, k, k).wait_recv()
            value = red[r, stage, 0]
            for k in range(1, size):
                value = value + red[r, stage, k]
        return value

    def column(value, k):
        return jnp.sum(jnp.where(tcol == k, value, 0.0), axis=1, keepdims=True)

    def steps(value):
        rho, mu, nu, xi = (column(value, k) for k in range(4))
        alpha = rho / mu
        rho1 = rho - 2.0 * alpha * mu + alpha * alpha * nu
        beta1 = 1.0 + rho1 / rho
        curve = beta1 * beta1 * mu - 2.0 * alpha * beta1 * nu + alpha * alpha * xi
        alpha1 = rho1 / curve
        return alpha + alpha1 * beta1, -alpha * alpha1

    first(0)
    second(0)
    first(1)
    third(0)
    value = sum_over_vox(0)
    c1, c2 = steps(value)
    predicted = column(value, 4) + c1 * column(value, 5) + c2 * column(value, 6)
    observed = jnp.zeros((PC, 1), jnp.float32)
    for p in range(PC):
        observed = jnp.where(trow[:, 0:1] == p, obs[p], observed)
    kc[0] = jnp.broadcast_to(c1, (PC, N))
    kc[1] = jnp.broadcast_to(c2, (PC, N))
    kc[2] = jnp.broadcast_to(data_weight * (predicted - observed), (PC, N))
    pred_out[...] = jnp.broadcast_to(predicted, (PC, N))
    second(1)
    third(1)
    value = sum_over_vox(1)
    c1, c2 = steps(value)
    kc[3] = jnp.broadcast_to(c1, (PC, N))
    kc[4] = jnp.broadcast_to(c2, (PC, N))

    @pl.loop(0, PC)
    def _(p):
        fields = []
        for s, (own_d, k1, k2) in enumerate((
            ([d0.at[0, p, 0], d0.at[0, p, 1]], 0, 1),
            ([dc.at[p, 0], dc.at[p, 1]], 3, 4),
        )):
            m1, m2 = kc[k1, pl.ds(p, 1), :], kc[k2, pl.ds(p, 1), :]
            fields.append((
                xh[s, 0, p] + m1 * dh[s, 0, p] + m2 * wh[s, 0, p],
                warm[s][0, p] + m1 * own_d[0][...] + m2 * w0[s, p, 0],
                warm[s][1, p] + m1 * own_d[1][...] + m2 * w0[s, p, 1],
                xh[s, 1, p] + m1 * dh[s, 1, p] + m2 * wh[s, 1, p],
            ))
        f, a = fields
        for k in range(3):
            acc[k] += (f[k + 1] - f[k]) * (a[k + 1] - a[k])
        for k in range(2):
            x, y = f[k + 1], a[k + 1]
            acc[3 + k] += (up_row(x) - x) * (up_row(y) - y)
            acc[5 + k] += (up_col(x) - x) * (up_col(y) - y)

    for plane in range(2):
        lo, hi = acc[plane], acc[plane + 1]
        lo = lo * lo_open if plane == 0 else lo
        hi = hi * hi_open if plane == 1 else hi
        px = jnp.where(rows < N - 1, acc[3 + plane], 0.0)
        py = jnp.where(cols < N - 1, acc[5 + plane], 0.0)
        gb[plane] = -0.5 * ((lo + hi) + (px + down_row(px)) + (py + down_col(py)))

    def part(k):
        return pl.ds(pl.multiple_of(k * chunk, chunk), chunk)

    def rs_copy(k, slot):
        return pltpu.make_async_remote_copy(
            gb.at[:, part(k), :], rsb.at[slot], rs_s.at[k], rs_r.at[slot],
            device_id=(k, v), device_id_type=MESH,
        )

    def ag_copy(k, slot):
        return pltpu.make_async_remote_copy(
            agb.at[:, part(slot), :], agb.at[:, part(slot), :], ag_s.at[k], ag_r.at[slot],
            device_id=(k, v), device_id_type=MESH,
        )

    others = [lax.rem(q + j, npat) for j in range(1, npat)]
    for k in others:
        rs_copy(k, q).start()
    rsb[q] = gb[:, part(q), :]
    for k in others:
        rs_copy(k, k).wait_recv()
    whole = rsb[0]
    for k in range(1, npat):
        whole = whole + rsb[k]
    agb[:, part(q), :] = whole
    for k in others:
        ag_copy(k, q).start()
    for k in others:
        ag_copy(k, k).wait_recv()
    grad_out[...] = agb[...]

    @pl.when(has_hi)
    def _():
        sig_copy(0).wait_send()

    @pl.when(has_lo)
    def _():
        sig_copy(1).wait_send()

    @pl.loop(0, PC)
    def _(p):
        for stage in range(3):
            for s in range(2):
                @pl.when(has_hi)
                def _():
                    halo_copy(stage, s, 0, p).wait_send()

                @pl.when(has_lo)
                def _():
                    halo_copy(stage, s, 1, p).wait_send()

    for r in range(2):
        for stage in range(2):
            for j in range(1, sizes[stage]):
                sum_copy(r, stage, lax.rem(rank[stage] + j, sizes[stage]), rank[stage]).wait_send()
    for k in others:
        rs_copy(k, q).wait_send()
        ag_copy(k, q).wait_send()


def solution(mesh):
    npat, layers = mesh.shape["pat"], mesh.shape["vox"]
    group = 8 if layers >= 64 else 2

    def per_device(conductivity, warm_forward, warm_adjoint, electrodes, patterns, observed):
        planes = conductivity.shape[0]
        strength = 2.0 * math.sqrt(layers * planes * PLANE)
        vmem = pl.BlockSpec(memory_space=pltpu.VMEM)
        smem = pl.BlockSpec(memory_space=pltpu.SMEM)
        f32 = jnp.float32
        dma = pltpu.SemaphoreType.DMA
        groups = layers // group
        widest = max(group, groups)
        gradient, predicted = pl.pallas_call(
            functools.partial(kernel, npat, layers, group, strength),
            out_shape=(
                jax.ShapeDtypeStruct((2, N, N), f32),
                jax.ShapeDtypeStruct((PC, N), f32),
            ),
            in_specs=[vmem, vmem, vmem, smem, smem, smem],
            out_specs=(vmem, vmem),
            scratch_shapes=[
                pltpu.VMEM((2, 2, N, N), f32),
                pltpu.VMEM((2, 2, PC, N, N), f32),
                pltpu.VMEM((2, 2, PC, N, N), f32),
                pltpu.VMEM((2, 2, PC, N, N), f32),
                pltpu.VMEM((2, PC, 2, N, N), f32),
                pltpu.VMEM((2, PC, 2, N, N), f32),
                pltpu.VMEM((PC, 2, N, N), f32),
                pltpu.VMEM((8, 2, N, N), f32),
                pltpu.VMEM((2, N, N), f32),
                pltpu.VMEM((7, N, N), f32),
                pltpu.VMEM((2, PC, N), f32),
                pltpu.VMEM((2, 2, widest, PC, N), f32),
                pltpu.VMEM((5, PC, N), f32),
                pltpu.VMEM((2, N, N), f32),
                pltpu.VMEM((npat, 2, N // npat, N), f32),
                pltpu.VMEM((2, N, N), f32),
                dma((2,)),
                dma((2,)),
                dma((3, 2, 2, PC)),
                dma((3, 2, 2, PC)),
                dma((2, 2, widest)),
                dma((2, 2, widest)),
                dma((npat,)),
                dma((npat,)),
                dma((npat,)),
                dma((npat,)),
            ],
            compiler_params=pltpu.CompilerParams(
                collective_id=0, has_side_effects=True, vmem_limit_bytes=48 * 2**20
            ),
            name="ert_gradient",
        )(conductivity, warm_forward, warm_adjoint, electrodes, patterns, observed)
        return gradient, predicted[:, 0]

    in_specs = (
        P("vox", None, None),
        P("vox", "pat", None, None),
        P("vox", "pat", None, None),
        P(),
        P("pat", None),
        P("pat"),
    )
    return jax.shard_map(
        per_device,
        mesh=mesh,
        in_specs=in_specs,
        out_specs=(P("vox", None, None), P("pat")),
        check_vma=False,
    )
```

time: 1670 us -> 122 us (0.07)
  blocking collectives: 1360 us -> 0 us
  waiting for transfers between devices: 173 us -> 0 us
  Pallas kernels: 0 us -> 116 us
  starting transfers between devices: 76.3 us -> 0 us
  other arithmetic: 31.2 us -> 0 us
    psum x7 -> x0, blocking collectives: 1360 us -> none  [the longest x6 1160 us: pattern_sum(): return lax.psum(local_terms, 'vox')]
    psum x1 -> x0, waiting for transfers between devices: 124 us -> none  [per_device(): gradient = lax.psum(local_gradient, 'pat')]
    pallas_call x0 -> x1, Pallas kernels: none -> 116 us  [per_device(): pl.pallas_call(functools.partial(kernel, npat, layers, group, strength),...]
    ppermute x16 -> x0, starting transfers between devices: 76.3 us -> none  [the longest x8 58.3 us: extended(): lax.ppermute(lax.slice_in_dim(block, 0, width, axis=dim), axis, backward)]
    ppermute x16 -> x0, waiting for transfers between devices: 49 us -> none  [the longest x8 26.1 us: extended(): lax.ppermute(lax.slice_in_dim(block, block.shape[dim] - width, None, axis...]
  transfers between devices with their start and end apart: 17 -> 0, of which waited for: 12 -> 0; matrix products, arithmetic and copies ran while one was open for 1% -> 0% of each run, Pallas kernels for 0% -> 0%
where the time goes in v1:
time: 122 us
  Pallas kernels  116 us (95%)
  local copies, waits for them, and re-layouts  5.41 us (4%)
    pallas_call x1, Pallas kernels, per_device(): pl.pallas_call(functools.partial(kernel, npat, layers, group, strength),...  116 us
    unnamed x12, local copies, waits for them, and re-layouts  4.78 us

profile of v1, /device:TPU:8, one launch (start us, length us, event | category | flops | bytes accessed | tf_op | source)
XLA Modules:
  0.0 122.2 jit_solution(15342450191573761433)
XLA Ops:
  0.6 0.0 copy-start.4
  0.6 0.0 copy-start.3
  0.7 0.8 copy.9.pats
  1.4 0.0 copy-done.4
  1.4 0.0 copy-done.3
  1.4 0.0 copy-start
  1.4 1.2 %copy-done = f32[2,8,128,128]{3,2,1,0:T(8,128)S(1)} copy-done((f32[2,8,128,128]{3,2,1,0:T(8,128)S(1)}, f32[2,8,128,128]{3,2,1,0:T(8,128)}, u32[]{:S(2)}) %copy-start) | copy-done | bytes 1048600
  2.6 0.0 copy-start.1
  2.7 1.2 %copy-done.1 = f32[2,8,128,128]{3,2,1,0:T(8,128)S(1)} copy-done((f32[2,8,128,128]{3,2,1,0:T(8,128)S(1)}, f32[2,8,128,128]{3,2,1,0:T(8,128)}, u32[]{:S(2)}) %copy-start.1) | copy-done | bytes 1048600
  3.9 0.0 copy-start.2
  3.9 0.9 copy-done.2
  4.8 116.1 %ert_gradient.1 = (f32[2,128,128]{2,1,0:T(8,128)S(1)}, f32[8,128]{1,0:T(8,128)S(1)}) custom-call(f32[2,128,128]{2,1,0:T(8,128)S(1)} %copy-done.2, f32[2,8,128,128]{3,2,1,0:T(8,128)S(1)} %copy-done, f32[2,8,128,128]{3,2,1,0:T(8,128)S(1)} %copy-done.1, s32[128]{0:T(128)S(1)} %copy-done.3, s32[8,4]{1,0:T(8,128)S(1)} %copy.9.pats, f32[8]{0:T(128)S(1)} %copy-done.4), custom_call_target="tpu_custom_call" | custom-call | tf_op jit(solution)/shard_map/ert_gradient/pallas_call | solution.py:472
  120.9 0.6 slice_reduce_fusion
  121.6 0.7 copy.11
Async XLA Ops:
  0.6 0.8 copy-start.4
  0.6 0.8 copy-start.3
  1.4 1.2 %copy-start = (f32[2,8,128,128]{3,2,1,0:T(8,128)S(1)}, f32[2,8,128,128]{3,2,1,0:T(8,128)}, u32[]{:S(2)}) copy-start(f32[2,8,128,128]{3,2,1,0:T(8,128)} %wf.1) | copy-start | bytes 3145732
  2.6 1.2 %copy-start.1 = (f32[2,8,128,128]{3,2,1,0:T(8,128)S(1)}, f32[2,8,128,128]{3,2,1,0:T(8,128)}, u32[]{:S(2)}) copy-start(f32[2,8,128,128]{3,2,1,0:T(8,128)} %wa.1) | copy-start | bytes 3145732
  3.9 0.9 copy-start.2

commit v2 on v1

v2 whole, which is shorter than its diff:
```python
import functools
import math

import jax
import jax.numpy as jnp
from jax import lax
from jax.experimental import pallas as pl
from jax.experimental.pallas import tpu as pltpu
from jax.sharding import PartitionSpec as P

MESH = pl.DeviceIdType.MESH
LEAK = 0.05
N = 128
PLANE = N * N
PC = 8

ZL, ZH, XM, XP, YM, YP = range(6)
F_RHO, F_MU, F_NU, F_XI, F_X, F_D, F_W = range(7)
YY, GY, GG = 7, 11, 15


def up_row(x):
    return pltpu.roll(x, N - 1, 0)


def down_row(x):
    return pltpu.roll(x, 1, 0)


def up_col(x):
    return pltpu.roll(x, N - 1, 1)


def down_col(x):
    return pltpu.roll(x, 1, 1)


def total(x):
    part = jnp.sum(x.reshape(N // 8, 8, N), axis=0)
    return jnp.sum(jnp.sum(part, axis=1, keepdims=True), axis=0, keepdims=True)


def kernel(
    npat,
    layers,
    group,
    strength,
    cond_in,
    wf_in,
    wa_in,
    elec,
    pats,
    obs,
    grad_out,
    pred_out,
    cond,
    warm,
    sh,
    fh,
    xh,
    dh,
    wh,
    d0,
    w0,
    gd,
    gw,
    rb,
    co,
    dg,
    di,
    acc,
    tile,
    red,
    kc,
    gb,
    rsb,
    agb,
    in_s,
    sig_s,
    sig_r,
    hs,
    hr,
    rr,
    rq,
    red_s,
    red_r,
    rs_s,
    rs_r,
    ag_s,
    ag_r,
):
    q = lax.axis_index("pat")
    v = lax.axis_index("vox")
    last = layers - 1
    has_lo = v > 0
    has_hi = v < last
    groups = layers // group
    rank = (lax.rem(v, group), v // group)
    sizes = (group, groups)
    data_weight = 0.1 * strength
    chunk = N // npat
    lower, upper = layers // 2 - 1, layers // 2
    inner = (q >= npat // 2 - 1) & (q <= npat // 2) if npat > 2 else q == 0
    crossing = ((lower, upper, 0), (upper, lower, last))

    local = [
        pltpu.make_async_copy(cond_in, cond, in_s.at[0]),
        pltpu.make_async_copy(wf_in, warm.at[0], in_s.at[1]),
        pltpu.make_async_copy(wa_in, warm.at[1], in_s.at[2]),
    ]

    def member(stage, k):
        return (v // group) * group + k if stage == 0 else k * group + lax.rem(v, group)

    barrier = pltpu.get_barrier_semaphore()

    def greet(device):
        pl.semaphore_signal(barrier, inc=1, device_id=device, device_id_type=MESH)

    @pl.when(has_lo)
    def _():
        greet((q, v - 1))

    @pl.when(has_hi)
    def _():
        greet((q, v + 1))

    expected = has_lo.astype(jnp.int32) + has_hi.astype(jnp.int32)
    for source, target, via in crossing:
        on_path = inner & ((v == source) | (v == target))

        @pl.when(on_path)
        def _():
            greet((q, via))

        @pl.when(inner & (v == via))
        def _():
            greet((q, source))
            greet((q, target))

        expected = expected + on_path.astype(jnp.int32)
        expected = expected + 2 * (inner & (v == via)).astype(jnp.int32)

    for stage in range(2):
        for j in range(1, sizes[stage]):
            greet((q, member(stage, lax.rem(rank[stage] + j, sizes[stage]))))
    for j in range(1, npat):
        greet((lax.rem(q + j, npat), v))

    for copy in local:
        copy.start()

    rows = lax.broadcasted_iota(jnp.int32, (N, N), 0)
    cols = lax.broadcasted_iota(jnp.int32, (N, N), 1)
    cell = rows * N + cols
    trow = lax.broadcasted_iota(jnp.int32, (PC, N), 0)
    tcol = lax.broadcasted_iota(jnp.int32, (PC, N), 1)
    blank = jnp.zeros((N, N), jnp.float32)

    for d, outside in enumerate((jnp.logical_not(has_lo), jnp.logical_not(has_hi))):
        @pl.when(outside)
        def _():
            sh[d, 0] = blank
            sh[d, 1] = blank
            fh[d] = blank

            @pl.loop(0, PC)
            def _(p):
                for s in range(2):
                    for h in (xh, dh, wh):
                        h[s, d, p] = blank

    tile[...] = jnp.zeros((PC, N), jnp.float32)
    for k in range(7):
        acc[k] = blank

    def neighbour(d):
        return (q, v + 1 - 2 * d)

    def sig_copy(kind, d):
        plane = (1 - d, d)[kind] if kind < 2 else None
        src = di.at[2 + d] if kind == 2 else cond.at[plane]
        dst = fh.at[d] if kind == 2 else sh.at[d, plane]
        return pltpu.make_async_remote_copy(
            src, dst, sig_s.at[kind, d], sig_r.at[kind, d],
            device_id=neighbour(d), device_id_type=MESH,
        )

    def outgoing(stage, s, d, p):
        plane = 1 - d
        if stage == 0:
            return warm.at[s, plane, p]
        return (d0 if stage == 1 else w0).at[s, p, plane]

    def incoming(stage, s, d, p):
        return (xh, dh, wh)[stage].at[s, d, p]

    def halo_copy(stage, s, d, p):
        return pltpu.make_async_remote_copy(
            outgoing(stage, s, d, p), incoming(stage, s, d, p),
            hs.at[stage, s, d, p], hr.at[stage, s, d, p],
            device_id=neighbour(d), device_id_type=MESH,
        )

    def detour_in(stage, s, d, p):
        at = s * (PC // 2) + p // 2
        return pltpu.make_async_remote_copy(
            outgoing(stage, s, d, p), rb.at[stage, at],
            hs.at[stage, s, d, p], rr.at[stage, at],
            device_id=(q, crossing[d][2]), device_id_type=MESH,
        )

    def detour_out(stage, s, d, p):
        at = s * (PC // 2) + p // 2
        return pltpu.make_async_remote_copy(
            rb.at[stage, at], incoming(stage, s, d, p),
            rq.at[stage, at], hr.at[stage, s, d, p],
            device_id=(q, crossing[d][1]), device_id_type=MESH,
        )

    exists = (has_hi, has_lo)

    def both(fn):
        for d in range(2):
            @pl.when(exists[d])
            def _():
                fn(d)

    def both_in(fn):
        for d in range(2):
            @pl.when(exists[1 - d])
            def _():
                fn(d)

    def send_halo(stage, s, p):
        odd = lax.rem(p, 2) == 1
        for d in range(2):
            around = inner & (v == crossing[d][0]) & odd

            @pl.when(exists[d] & jnp.logical_not(around))
            def _():
                halo_copy(stage, s, d, p).start()

            @pl.when(around)
            def _():
                detour_in(stage, s, d, p).start()

    def pass_on(stage, s, p):
        odd = lax.rem(p, 2) == 1
        for d in range(2):
            @pl.when(inner & (v == crossing[d][2]) & odd)
            def _():
                detour_in(stage, s, d, p).wait_recv()
                detour_out(stage, s, d, p).start()

    def await_halo(stage, s, p):
        both_in(lambda d: halo_copy(stage, s, d, p).wait_recv())

    for copy in local:
        copy.wait()
    partners = (sizes[0] - 1) + (sizes[1] - 1) + (npat - 1)
    pl.semaphore_wait(barrier, partners + expected)

    both(lambda d: sig_copy(0, d).start())
    for s in range(2):
        @pl.loop(0, PC)
        def _(p):
            send_halo(0, s, p)
    both(lambda d: sig_copy(1, d).start())

    lo_open = has_lo.astype(jnp.float32)
    hi_open = has_hi.astype(jnp.float32)

    def couple(k, s, below, above):
        xp = jnp.where(rows < N - 1, 0.5 * (s + up_row(s)), 0.0)
        yp = jnp.where(cols < N - 1, 0.5 * (s + up_col(s)), 0.0)
        xm, ym = down_row(xp), down_col(yp)
        diag = LEAK + (below + above) + (xp + xm) + (yp + ym)
        inv = 1.0 / diag
        for at, value in ((ZL, below), (ZH, above), (XM, xm), (XP, xp), (YM, ym), (YP, yp)):
            co[at, k] = value * inv
        if k in (1, 2):
            dg[k - 1] = diag
        di[k + 1] = inv

    both_in(lambda d: sig_copy(0, d).wait_recv())
    couple(1, cond[0], 0.5 * (cond[0] + sh[0, 1]) * lo_open, 0.5 * (cond[0] + cond[1]))
    couple(2, cond[1], 0.5 * (cond[0] + cond[1]), 0.5 * (cond[1] + sh[1, 0]) * hi_open)
    both(lambda d: sig_copy(2, d).start())

    def apply(k, x, below, above):
        y = co[ZL, k] * below + co[ZH, k] * above
        y = y + co[XM, k] * down_row(x) + co[XP, k] * up_row(x)
        y = y + co[YM, k] * down_col(x) + co[YP, k] * up_col(x)
        return x - y

    def difference(p, first, second, plane, scale):
        here = (2 * v + plane) * PLANE
        plus = jnp.where(cell == elec[pats[first, p]] - here, scale, 0.0)
        return plus - jnp.where(cell == elec[pats[second, p]] - here, scale, 0.0)

    def probe(p, plane):
        return difference(p, 2, 3, plane, 1.0)

    def record(p, values):
        now = tile[...]
        for k, value in values:
            now = jnp.where((trow == p) & (tcol == k), value, now)
        tile[...] = now

    for s in range(2):
        @pl.loop(0, PC)
        def _(p):
            await_halo(0, s, p)
            a, b = warm[s, 0, p], warm[s, 1, p]
            e0 = -apply(1, a, xh[s, 0, p], b)
            e1 = -apply(2, b, a, xh[s, 1, p])
            if s == 0:
                e0 = e0 + difference(p, 0, 1, 0, strength) * di[2]
                e1 = e1 + difference(p, 0, 1, 1, strength) * di[3]
            d0[s, p, 0] = e0
            d0[s, p, 1] = e1
            send_halo(1, s, p)
            g0, g1 = probe(p, 0), probe(p, 1)
            rho = total(dg[0] * e0 * e0 + dg[1] * e1 * e1)
            ge = total(g0 * e0 + g1 * e1)
            if s == 0:
                record(p, ((F_RHO, rho), (F_D, ge), (F_X, total(g0 * a + g1 * b))))
            else:
                record(p, ((YY, rho), (GY, ge)))
            pass_on(0, s, p)

    both_in(lambda d: sig_copy(1, d).wait_recv())
    couple(0, sh[0, 1], 0.5 * (sh[0, 0] + sh[0, 1]), 0.5 * (cond[0] + sh[0, 1]) * lo_open)
    couple(3, sh[1, 0], 0.5 * (cond[1] + sh[1, 0]) * hi_open, 0.5 * (sh[1, 0] + sh[1, 1]))
    both_in(lambda d: sig_copy(2, d).wait_recv())
    di[0] = fh[0]
    di[5] = fh[1]

    @pl.loop(0, PC)
    def _(p):
        e = [probe(p, k - 2) * di[k] for k in range(6)]
        y = [apply(k, e[k + 1], e[k], e[k + 2]) for k in range(4)]
        for k in range(4):
            gd[p, k] = e[k + 1]
            gw[p, k] = y[k]
        z0, z1 = apply(1, y[1], y[0], y[2]), apply(2, y[2], y[1], y[3])
        g0, g1 = probe(p, 0), probe(p, 1)
        u0, u1 = dg[0] * y[1], dg[1] * y[2]
        record(p, (
            (GG, total(g0 * e[2] + g1 * e[3])),
            (GG + 1, total(g0 * y[1] + g1 * y[2])),
            (GG + 2, total(u0 * y[1] + u1 * y[2])),
            (GG + 3, total(u0 * z0 + u1 * z1)),
        ))

    for s in range(2):
        @pl.loop(0, PC)
        def _(p):
            await_halo(1, s, p)
            a, b = d0[s, p, 0], d0[s, p, 1]
            y0 = apply(1, a, dh[s, 0, p], b)
            y1 = apply(2, b, a, dh[s, 1, p])
            w0[s, p, 0] = y0
            w0[s, p, 1] = y1
            send_halo(2, s, p)
            u0, u1 = dg[0] * y0, dg[1] * y1
            mu = total(u0 * a + u1 * b)
            nu = total(u0 * y0 + u1 * y1)
            gy = total(probe(p, 0) * y0 + probe(p, 1) * y1)
            if s == 0:
                record(p, ((F_MU, mu), (F_NU, nu), (F_W, gy)))
            else:
                cross = total(u0 * gw[p, 1] + u1 * gw[p, 2])
                record(p, ((YY + 1, mu), (YY + 2, nu), (GY + 1, gy), (GY + 2, cross)))
            pass_on(1, s, p)

    for s in range(2):
        @pl.loop(0, PC)
        def _(p):
            pass_on(2, s, p)
            await_halo(2, s, p)
            a, b = w0[s, p, 0], w0[s, p, 1]
            u0 = dg[0] * apply(1, a, wh[s, 0, p], b)
            u1 = dg[1] * apply(2, b, a, wh[s, 1, p])
            xi = total(a * u0 + b * u1)
            if s == 0:
                record(p, ((F_XI, xi),))
            else:
                cross = total(u0 * gw[p, 1] + u1 * gw[p, 2])
                record(p, ((YY + 3, xi), (GY + 3, cross)))

    def sum_copy(stage, k, slot):
        return pltpu.make_async_remote_copy(
            red.at[stage, slot], red.at[stage, slot],
            red_s.at[stage, k], red_r.at[stage, slot],
            device_id=(q, member(stage, k)), device_id_type=MESH,
        )

    value = tile[...]
    for stage in range(2):
        mine, size = rank[stage], sizes[stage]
        red[stage, mine] = value
        for j in range(1, size):
            sum_copy(stage, lax.rem(mine + j, size), mine).start()
        for j in range(1, size):
            k = lax.rem(mine + j, size)
            sum_copy(stage, k, k).wait_recv()
        value = red[stage, 0]
        for k in range(1, size):
            value = value + red[stage, k]

    def column(k):
        return jnp.sum(jnp.where(tcol == k, value, 0.0), axis=1, keepdims=True)

    def steps(rho, mu, nu, xi):
        alpha = rho / mu
        rho1 = rho - 2.0 * alpha * mu + alpha * alpha * nu
        beta1 = 1.0 + rho1 / rho
        curve = beta1 * beta1 * mu - 2.0 * alpha * beta1 * nu + alpha * alpha * xi
        alpha1 = rho1 / curve
        return alpha + alpha1 * beta1, -alpha * alpha1

    c1, c2 = steps(column(F_RHO), column(F_MU), column(F_NU), column(F_XI))
    predicted = column(F_X) + c1 * column(F_D) + c2 * column(F_W)
    observed = jnp.zeros((PC, 1), jnp.float32)
    for p in range(PC):
        observed = jnp.where(trow[:, 0:1] == p, obs[p], observed)
    weight = data_weight * (predicted - observed)
    e1, e2 = steps(*(
        column(YY + k) + weight * (2.0 * column(GY + k) + weight * column(GG + k))
        for k in range(4)
    ))
    for k, factor in enumerate((c1, c2, e1, e2, e1 * weight, e2 * weight)):
        kc[k] = jnp.broadcast_to(factor, (PC, N))
    wide = jnp.where(trow == tcol, predicted, 0.0)
    pred_out[...] = jnp.sum(wide, axis=0, keepdims=True)[:, :PC]

    @pl.loop(0, PC)
    def _(p):
        m = [kc[k, pl.ds(p, 1), :] for k in range(6)]

        def field(s, k):
            if k in (0, 3):
                x, d, w = (h[s, k // 3, p] for h in (xh, dh, wh))
            else:
                x, d, w = warm[s, k - 1, p], d0[s, p, k - 1], w0[s, p, k - 1]
            out = x + m[2 * s] * d + m[2 * s + 1] * w
            if s == 1:
                out = out + m[4] * gd[p, k] + m[5] * gw[p, k]
            return out

        f = [field(0, k) for k in range(4)]
        a = [field(1, k) for k in range(4)]
        for k in range(3):
            acc[k] += (f[k + 1] - f[k]) * (a[k + 1] - a[k])
        for k in range(2):
            x, y = f[k + 1], a[k + 1]
            acc[3 + k] += (up_row(x) - x) * (up_row(y) - y)
            acc[5 + k] += (up_col(x) - x) * (up_col(y) - y)

    for plane in range(2):
        lo, hi = acc[plane], acc[plane + 1]
        lo = lo * lo_open if plane == 0 else lo
        hi = hi * hi_open if plane == 1 else hi
        px = jnp.where(rows < N - 1, acc[3 + plane], 0.0)
        py = jnp.where(cols < N - 1, acc[5 + plane], 0.0)
        gb[plane] = -0.5 * ((lo + hi) + (px + down_row(px)) + (py + down_col(py)))

    def part(k):
        return pl.ds(pl.multiple_of(k * chunk, chunk), chunk)

    def rs_copy(k, slot):
        return pltpu.make_async_remote_copy(
            gb.at[:, part(k), :], rsb.at[slot], rs_s.at[k], rs_r.at[slot],
            device_id=(k, v), device_id_type=MESH,
        )

    def ag_copy(k, slot):
        return pltpu.make_async_remote_copy(
            agb.at[:, part(slot), :], agb.at[:, part(slot), :], ag_s.at[k], ag_r.at[slot],
            device_id=(k, v), device_id_type=MESH,
        )

    others = [lax.rem(q + j, npat) for j in range(1, npat)]
    for k in others:
        rs_copy(k, q).start()
    rsb[q] = gb[:, part(q), :]
    for k in others:
        rs_copy(k, k).wait_recv()
    whole = rsb[0]
    for k in range(1, npat):
        whole = whole + rsb[k]
    agb[:, part(q), :] = whole
    for k in others:
        ag_copy(k, q).start()
    for k in others:
        ag_copy(k, k).wait_recv()
    grad_out[...] = agb[...]

    for kind in range(3):
        both(lambda d: sig_copy(kind, d).wait_send())

    @pl.loop(0, PC)
    def _(p):
        for stage in range(3):
            for s in range(2):
                both(lambda d: halo_copy(stage, s, d, p).wait_send())
                for d in range(2):
                    @pl.when(inner & (v == crossing[d][2]) & (lax.rem(p, 2) == 1))
                    def _():
                        detour_out(stage, s, d, p).wait_send()

    for stage in range(2):
        for j in range(1, sizes[stage]):
            sum_copy(stage, lax.rem(rank[stage] + j, sizes[stage]), rank[stage]).wait_send()
    for k in others:
        rs_copy(k, q).wait_send()
        ag_copy(k, q).wait_send()


def solution(mesh):
    npat, layers = mesh.shape["pat"], mesh.shape["vox"]
    group = 8 if layers >= 64 else 2

    def per_device(conductivity, warm_forward, warm_adjoint, electrodes, patterns, observed):
        planes = conductivity.shape[0]
        strength = 2.0 * math.sqrt(layers * planes * PLANE)
        vmem = pl.BlockSpec(memory_space=pltpu.VMEM)
        smem = pl.BlockSpec(memory_space=pltpu.SMEM)
        hbm = pl.BlockSpec(memory_space=pltpu.HBM)
        f32 = jnp.float32
        dma = pltpu.SemaphoreType.DMA
        groups = layers // group
        widest = max(group, groups)
        gradient, predicted = pl.pallas_call(
            functools.partial(kernel, npat, layers, group, strength),
            out_shape=(
                jax.ShapeDtypeStruct((2, N, N), f32),
                jax.ShapeDtypeStruct((1, PC), f32),
            ),
            in_specs=[hbm, hbm, hbm, smem, smem, smem],
            out_specs=(vmem, vmem),
            scratch_shapes=[
                pltpu.VMEM((2, N, N), f32),
                pltpu.VMEM((2, 2, PC, N, N), f32),
                pltpu.VMEM((2, 2, N, N), f32),
                pltpu.VMEM((2, N, N), f32),
                pltpu.VMEM((2, 2, PC, N, N), f32),
                pltpu.VMEM((2, 2, PC, N, N), f32),
                pltpu.VMEM((2, 2, PC, N, N), f32),
                pltpu.VMEM((2, PC, 2, N, N), f32),
                pltpu.VMEM((2, PC, 2, N, N), f32),
                pltpu.VMEM((PC, 4, N, N), f32),
                pltpu.VMEM((PC, 4, N, N), f32),
                pltpu.VMEM((3, PC, N, N), f32),
                pltpu.VMEM((6, 4, N, N), f32),
                pltpu.VMEM((2, N, N), f32),
                pltpu.VMEM((6, N, N), f32),
                pltpu.VMEM((7, N, N), f32),
                pltpu.VMEM((PC, N), f32),
                pltpu.VMEM((2, widest, PC, N), f32),
                pltpu.VMEM((6, PC, N), f32),
                pltpu.VMEM((2, N, N), f32),
                pltpu.VMEM((npat, 2, N // npat, N), f32),
                pltpu.VMEM((2, N, N), f32),
                dma((3,)),
                dma((3, 2)),
                dma((3, 2)),
                dma((3, 2, 2, PC)),
                dma((3, 2, 2, PC)),
                dma((3, PC)),
                dma((3, PC)),
                dma((2, widest)),
                dma((2, widest)),
                dma((npat,)),
                dma((npat,)),
                dma((npat,)),
                dma((npat,)),
            ],
            compiler_params=pltpu.CompilerParams(
                collective_id=0, has_side_effects=True, vmem_limit_bytes=58 * 2**20
            ),
            name="ert_gradient",
        )(conductivity, warm_forward, warm_adjoint, electrodes, patterns.T, observed)
        return gradient, predicted.reshape(PC)

    in_specs = (
        P("vox", None, None),
        P("vox", "pat", None, None),
        P("vox", "pat", None, None),
        P(),
        P("pat", None),
        P("pat"),
    )
    return jax.shard_map(
        per_device,
        mesh=mesh,
        in_specs=in_specs,
        out_specs=(P("vox", None, None), P("pat")),
        check_vma=False,
    )
```

time: 122 us -> 95.6 us (0.78)
  Pallas kernels: 116 us -> 92.6 us
  local copies, waits for them, and re-layouts: 5.41 us -> 2.08 us
    pallas_call x1, Pallas kernels: 116 us -> 92.6 us  [per_device(): pl.pallas_call(functools.partial(kernel, npat, layers, group, strength),...]
    unnamed x12 -> x4, local copies, waits for them, and re-layouts: 4.78 us -> 2.08 us
where the time goes in v2:
time: 95.6 us; the launch traced here: 95.3 us
  Pallas kernels  92.6 us (97%)
  local copies, waits for them, and re-layouts  2.08 us (2%)
    pallas_call x1, Pallas kernels, per_device(): pl.pallas_call(functools.partial(kernel, npat, layers, group, strength),...  92.6 us
    unnamed x4, local copies, waits for them, and re-layouts  2.08 us

profile of v2, /device:TPU:8, one launch (start us, length us, event | category | flops | bytes accessed | tf_op | source)
XLA Modules:
  0.0 95.3 jit_solution(7713517696840462944)
XLA Ops:
  0.6 92.6 %ert_gradient.1 = (f32[2,128,128]{2,1,0:T(8,128)}, f32[1,8]{1,0:T(1,128)}) custom-call(f32[2,128,128]{2,1,0:T(8,128)} %cond_in.1, f32[2,8,128,128]{3,2,1,0:T(8,128)} %wf_in.1, f32[2,8,128,128]{3,2,1,0:T(8,128)} %wa_in.1, s32[128]{0:T(128)} %elec.1, s32[4,8]{1,0:T(4,128)} %bitcast.2, f32[8]{0:T(128)} %obs.1), custom_call_target="tpu_custom_call" | custom-call | tf_op jit(solution)/shard_map/ert_gradient/pallas_call | solution.py:536
  93.3 0.0 copy-start
  93.3 1.6 %copy.10 = f32[2,128,128]{2,1,0:T(8,128)} copy(f32[2,128,128]{2,1,0:T(8,128)} %get-tuple-element.8) | data formatting | bytes 262144
  94.8 0.0 copy-done
  94.8 0.5 copy.11
Async XLA Ops:
  93.3 1.6 %copy-start = (f32[1,8]{1,0:T(1,128)S(1)}, f32[1,8]{1,0:T(1,128)}, u32[]{:S(2)}) copy-start(f32[1,8]{1,0:T(1,128)} %get-tuple-element.5) | copy-start | bytes 100

commit v3 on v2

--- a/solution.py
+++ b/solution.py
@@ -13,6 +13,7 @@
 N = 128
 PLANE = N * N
 PC = 8
+PIECES = 8
 
 ZL, ZH, XM, XP, YM, YP = range(6)
 F_RHO, F_MU, F_NU, F_XI, F_X, F_D, F_W = range(7)
@@ -73,8 +74,10 @@
     red,
     kc,
     gb,
-    rsb,
-    agb,
+    lb_outer,
+    lb_inner,
+    half,
+    grad,
     in_s,
     sig_s,
     sig_r,
@@ -84,11 +87,10 @@
     rq,
     red_s,
     red_r,
-    rs_s,
-    rs_r,
-    ag_s,
-    ag_r,
+    ls,
+    lr,
 ):
+    lb = (lb_outer, lb_inner)
     q = lax.axis_index("pat")
     v = lax.axis_index("vox")
     last = layers - 1
@@ -98,10 +100,13 @@
     rank = (lax.rem(v, group), v // group)
     sizes = (group, groups)
     data_weight = 0.1 * strength
-    chunk = N // npat
     lower, upper = layers // 2 - 1, layers // 2
-    inner = (q >= npat // 2 - 1) & (q <= npat // 2) if npat > 2 else q == 0
-    crossing = ((lower, upper, 0), (upper, lower, last))
+    middle = npat // 2
+    inner = (q >= middle - 1) & (q <= middle) if npat > 2 else q == 0
+    crossing = (
+        (lower, upper, 0, inner),
+        (upper, lower, last, jnp.logical_not(inner)),
+    )
 
     local = [
         pltpu.make_async_copy(cond_in, cond, in_s.at[0]),
@@ -126,27 +131,35 @@
         greet((q, v + 1))
 
     expected = has_lo.astype(jnp.int32) + has_hi.astype(jnp.int32)
-    for source, target, via in crossing:
-        on_path = inner & ((v == source) | (v == target))
+    for source, target, via, taken in crossing:
+        on_path = taken & ((v == source) | (v == target))
 
         @pl.when(on_path)
         def _():
             greet((q, via))
 
-        @pl.when(inner & (v == via))
+        @pl.when(taken & (v == via))
         def _():
             greet((q, source))
             greet((q, target))
 
         expected = expected + on_path.astype(jnp.int32)
-        expected = expected + 2 * (inner & (v == via)).astype(jnp.int32)
+        expected = expected + 2 * (taken & (v == via)).astype(jnp.int32)
 
     for stage in range(2):
         for j in range(1, sizes[stage]):
             greet((q, member(stage, lax.rem(rank[stage] + j, sizes[stage]))))
-    for j in range(1, npat):
-        greet((lax.rem(q + j, npat), v))
-
+    below, above = q > 0, q < npat - 1
+
+    @pl.when(below)
+    def _():
+        greet((q - 1, v))
+
+    @pl.when(above)
+    def _():
+        greet((q + 1, v))
+
+    expected = expected + below.astype(jnp.int32) + above.astype(jnp.int32)
     for copy in local:
         copy.start()
 
@@ -203,7 +216,7 @@
         )
 
     def detour_in(stage, s, d, p):
-        at = s * (PC // 2) + p // 2
+        at = s * PC + p
         return pltpu.make_async_remote_copy(
             outgoing(stage, s, d, p), rb.at[stage, at],
             hs.at[stage, s, d, p], rr.at[stage, at],
@@ -211,7 +224,7 @@
         )
 
     def detour_out(stage, s, d, p):
-        at = s * (PC // 2) + p // 2
+        at = s * PC + p
         return pltpu.make_async_remote_copy(
             rb.at[stage, at], incoming(stage, s, d, p),
             rq.at[stage, at], hr.at[stage, s, d, p],
@@ -233,9 +246,8 @@
                 fn(d)
 
     def send_halo(stage, s, p):
-        odd = lax.rem(p, 2) == 1
         for d in range(2):
-            around = inner & (v == crossing[d][0]) & odd
+            around = crossing[d][3] & (v == crossing[d][0])
 
             @pl.when(exists[d] & jnp.logical_not(around))
             def _():
@@ -246,9 +258,8 @@
                 detour_in(stage, s, d, p).start()
 
     def pass_on(stage, s, p):
-        odd = lax.rem(p, 2) == 1
         for d in range(2):
-            @pl.when(inner & (v == crossing[d][2]) & odd)
+            @pl.when(crossing[d][3] & (v == crossing[d][2]))
             def _():
                 detour_in(stage, s, d, p).wait_recv()
                 detour_out(stage, s, d, p).start()
@@ -258,7 +269,7 @@
 
     for copy in local:
         copy.wait()
-    partners = (sizes[0] - 1) + (sizes[1] - 1) + (npat - 1)
+    partners = (sizes[0] - 1) + (sizes[1] - 1)
     pl.semaphore_wait(barrier, partners + expected)
 
     both(lambda d: sig_copy(0, d).start())
@@ -467,36 +478,55 @@
         py = jnp.where(cols < N - 1, acc[5 + plane], 0.0)
         gb[plane] = -0.5 * ((lo + hi) + (px + down_row(px)) + (py + down_col(py)))
 
-    def part(k):
-        return pl.ds(pl.multiple_of(k * chunk, chunk), chunk)
-
-    def rs_copy(k, slot):
+    is_outer = (q == 0) | (q == npat - 1) if npat > 2 else q < 0
+    is_inner = jnp.logical_not(is_outer)
+    outward = jnp.where(q < middle, q - 1, q + 1)
+    inward = jnp.where(q < middle, q + 1, q - 1)
+    height = N // (PIECES // 2)
+
+    def line_copy(leg, j):
+        at = (j // (PIECES // 2), pl.ds(j % (PIECES // 2) * height, height))
+        src = (gb, half, grad)[leg].at[at]
+        dst = (lb[0], lb[1], grad)[leg].at[at]
         return pltpu.make_async_remote_copy(
-            gb.at[:, part(k), :], rsb.at[slot], rs_s.at[k], rs_r.at[slot],
-            device_id=(k, v), device_id_type=MESH,
+            src, dst, ls.at[leg, j], lr.at[leg, j],
+            device_id=(outward if leg == 2 else inward, v), device_id_type=MESH,
         )
 
-    def ag_copy(k, slot):
-        return pltpu.make_async_remote_copy(
-            agb.at[:, part(slot), :], agb.at[:, part(slot), :], ag_s.at[k], ag_r.at[slot],
-            device_id=(k, v), device_id_type=MESH,
-        )
-
-    others = [lax.rem(q + j, npat) for j in range(1, npat)]
-    for k in others:
-        rs_copy(k, q).start()
-    rsb[q] = gb[:, part(q), :]
-    for k in others:
-        rs_copy(k, k).wait_recv()
-    whole = rsb[0]
-    for k in range(1, npat):
-        whole = whole + rsb[k]
-    agb[:, part(q), :] = whole
-    for k in others:
-        ag_copy(k, q).start()
-    for k in others:
-        ag_copy(k, k).wait_recv()
-    grad_out[...] = agb[...]
+    def piece(j):
+        return j // (PIECES // 2), slice(j % (PIECES // 2) * height, (j % (PIECES // 2) + 1) * height)
+
+    @pl.when(is_outer)
+    def _():
+        for j in range(PIECES):
+            line_copy(0, j).start()
+        for j in range(PIECES):
+            line_copy(2, j).wait_recv()
+        for j in range(PIECES):
+            line_copy(0, j).wait_send()
+
+    @pl.when(is_inner)
+    def _():
+        for j in range(PIECES):
+            at = piece(j)
+            if npat > 2:
+                line_copy(0, j).wait_recv()
+                half[at] = gb[at] + lb[0][at]
+            else:
+                half[at] = gb[at]
+            line_copy(1, j).start()
+        for j in range(PIECES):
+            at = piece(j)
+            line_copy(1, j).wait_recv()
+            grad[at] = half[at] + lb[1][at]
+            if npat > 2:
+                line_copy(2, j).start()
+        for j in range(PIECES):
+            line_copy(1, j).wait_send()
+            if npat > 2:
+                line_copy(2, j).wait_send()
+
+    grad_out[...] = grad[...]
 
     for kind in range(3):
         both(lambda d: sig_copy(kind, d).wait_send())
@@ -507,16 +537,13 @@
             for s in range(2):
                 both(lambda d: halo_copy(stage, s, d, p).wait_send())
                 for d in range(2):
-                    @pl.when(inner & (v == crossing[d][2]) & (lax.rem(p, 2) == 1))
+                    @pl.when(crossing[d][3] & (v == crossing[d][2]))
                     def _():
                         detour_out(stage, s, d, p).wait_send()
 
     for stage in range(2):
         for j in range(1, sizes[stage]):
             sum_copy(stage, lax.rem(rank[stage] + j, sizes[stage]), rank[stage]).wait_send()
-    for k in others:
-        rs_copy(k, q).wait_send()
-        ag_copy(k, q).wait_send()
 
 
 def solution(mesh):
@@ -553,7 +580,7 @@
                 pltpu.VMEM((2, PC, 2, N, N), f32),
                 pltpu.VMEM((PC, 4, N, N), f32),
                 pltpu.VMEM((PC, 4, N, N), f32),
-                pltpu.VMEM((3, PC, N, N), f32),
+                pltpu.VMEM((3, 2 * PC, N, N), f32),
                 pltpu.VMEM((6, 4, N, N), f32),
                 pltpu.VMEM((2, N, N), f32),
                 pltpu.VMEM((6, N, N), f32),
@@ -562,21 +589,21 @@
                 pltpu.VMEM((2, widest, PC, N), f32),
                 pltpu.VMEM((6, PC, N), f32),
                 pltpu.VMEM((2, N, N), f32),
-                pltpu.VMEM((npat, 2, N // npat, N), f32),
+                pltpu.VMEM((2, N, N), f32),
+                pltpu.VMEM((2, N, N), f32),
+                pltpu.VMEM((2, N, N), f32),
                 pltpu.VMEM((2, N, N), f32),
                 dma((3,)),
                 dma((3, 2)),
                 dma((3, 2)),
                 dma((3, 2, 2, PC)),
                 dma((3, 2, 2, PC)),
-                dma((3, PC)),
-                dma((3, PC)),
+                dma((3, 2 * PC)),
+                dma((3, 2 * PC)),
                 dma((2, widest)),
                 dma((2, widest)),
-                dma((npat,)),
-                dma((npat,)),
-                dma((npat,)),
-                dma((npat,)),
+                dma((3, PIECES)),
+                dma((3, PIECES)),
             ],
             compiler_params=pltpu.CompilerParams(
                 collective_id=0, has_side_effects=True, vmem_limit_bytes=58 * 2**20

time: 95.6 us -> 87.4 us (0.914)
  Pallas kernels: 92.6 us -> 84.5 us
    pallas_call x1, Pallas kernels: 92.6 us -> 84.5 us  [per_device(): pl.pallas_call(functools.partial(kernel, npat, layers, group, strength),...]
where the time goes in v3:
time: 87.4 us; the launch traced here: 87.2 us
  Pallas kernels  84.5 us (97%)
  local copies, waits for them, and re-layouts  2.08 us (2%)
    pallas_call x1, Pallas kernels, per_device(): pl.pallas_call(functools.partial(kernel, npat, layers, group, strength),...  84.5 us
    unnamed x4, local copies, waits for them, and re-layouts  2.08 us

profile of v3, /device:TPU:8, one launch (start us, length us, event | category | flops | bytes accessed | tf_op | source)
XLA Modules:
  0.0 87.2 jit_solution(9066188611350470856)
XLA Ops:
  0.6 84.5 %ert_gradient.1 = (f32[2,128,128]{2,1,0:T(8,128)}, f32[1,8]{1,0:T(1,128)}) custom-call(f32[2,128,128]{2,1,0:T(8,128)} %cond_in.1, f32[2,8,128,128]{3,2,1,0:T(8,128)} %wf_in.1, f32[2,8,128,128]{3,2,1,0:T(8,128)} %wa_in.1, s32[128]{0:T(128)} %elec.1, s32[4,8]{1,0:T(4,128)} %bitcast.2, f32[8]{0:T(128)} %obs.1), custom_call_target="tpu_custom_call" | custom-call | tf_op jit(solution)/shard_map/ert_gradient/pallas_call | solution.py:563
  85.1 0.0 copy-start
  85.1 1.6 %copy.10 = f32[2,128,128]{2,1,0:T(8,128)} copy(f32[2,128,128]{2,1,0:T(8,128)} %get-tuple-element.8) | data formatting | bytes 262144
  86.7 0.0 copy-done
  86.7 0.5 copy.11
Async XLA Ops:
  85.1 1.6 %copy-start = (f32[1,8]{1,0:T(1,128)S(1)}, f32[1,8]{1,0:T(1,128)}, u32[]{:S(2)}) copy-start(f32[1,8]{1,0:T(1,128)} %get-tuple-element.5) | copy-start | bytes 100

commit v4 on v3

--- a/solution.py
+++ b/solution.py
@@ -66,6 +66,7 @@
     gd,
     gw,
     rb,
+    sb,
     co,
     dg,
     di,
@@ -81,6 +82,8 @@
     in_s,
     sig_s,
     sig_r,
+    sig_rr,
+    sig_rq,
     hs,
     hr,
     rr,
@@ -190,13 +193,29 @@
     def neighbour(d):
         return (q, v + 1 - 2 * d)
 
+    def sig_ends(kind, d):
+        if kind == 2:
+            return di.at[2 + d], fh.at[d]
+        plane = (1 - d, d)[kind]
+        return cond.at[plane], sh.at[d, plane]
+
     def sig_copy(kind, d):
-        plane = (1 - d, d)[kind] if kind < 2 else None
-        src = di.at[2 + d] if kind == 2 else cond.at[plane]
-        dst = fh.at[d] if kind == 2 else sh.at[d, plane]
+        src, dst = sig_ends(kind, d)
         return pltpu.make_async_remote_copy(
             src, dst, sig_s.at[kind, d], sig_r.at[kind, d],
             device_id=neighbour(d), device_id_type=MESH,
+        )
+
+    def sig_in(kind, d):
+        return pltpu.make_async_remote_copy(
+            sig_ends(kind, d)[0], sb.at[kind], sig_s.at[kind, d], sig_rr.at[kind],
+            device_id=(q, crossing[d][2]), device_id_type=MESH,
+        )
+
+    def sig_out(kind, d):
+        return pltpu.make_async_remote_copy(
+            sb.at[kind], sig_ends(kind, d)[1], sig_rq.at[kind], sig_r.at[kind, d],
+            device_id=(q, crossing[d][1]), device_id_type=MESH,
         )
 
     def outgoing(stage, s, d, p):
@@ -245,6 +264,25 @@
             def _():
                 fn(d)
 
+    def send_sig(kind):
+        for d in range(2):
+            around = crossing[d][3] & (v == crossing[d][0])
+
+            @pl.when(exists[d] & jnp.logical_not(around))
+            def _():
+                sig_copy(kind, d).start()
+
+            @pl.when(around)
+            def _():
+                sig_in(kind, d).start()
+
+    def pass_sig(kind):
+        for d in range(2):
+            @pl.when(crossing[d][3] & (v == crossing[d][2]))
+            def _():
+                sig_in(kind, d).wait_recv()
+                sig_out(kind, d).start()
+
     def send_halo(stage, s, p):
         for d in range(2):
             around = crossing[d][3] & (v == crossing[d][0])
@@ -272,12 +310,12 @@
     partners = (sizes[0] - 1) + (sizes[1] - 1)
     pl.semaphore_wait(barrier, partners + expected)
 
-    both(lambda d: sig_copy(0, d).start())
+    send_sig(0)
     for s in range(2):
         @pl.loop(0, PC)
         def _(p):
             send_halo(0, s, p)
-    both(lambda d: sig_copy(1, d).start())
+    pass_sig(0)
 
     lo_open = has_lo.astype(jnp.float32)
     hi_open = has_hi.astype(jnp.float32)
@@ -297,7 +335,6 @@
     both_in(lambda d: sig_copy(0, d).wait_recv())
     couple(1, cond[0], 0.5 * (cond[0] + sh[0, 1]) * lo_open, 0.5 * (cond[0] + cond[1]))
     couple(2, cond[1], 0.5 * (cond[0] + cond[1]), 0.5 * (cond[1] + sh[1, 0]) * hi_open)
-    both(lambda d: sig_copy(2, d).start())
 
     def apply(k, x, below, above):
         y = co[ZL, k] * below + co[ZH, k] * above
@@ -341,29 +378,8 @@
                 record(p, ((YY, rho), (GY, ge)))
             pass_on(0, s, p)
 
-    both_in(lambda d: sig_copy(1, d).wait_recv())
-    couple(0, sh[0, 1], 0.5 * (sh[0, 0] + sh[0, 1]), 0.5 * (cond[0] + sh[0, 1]) * lo_open)
-    couple(3, sh[1, 0], 0.5 * (cond[1] + sh[1, 0]) * hi_open, 0.5 * (sh[1, 0] + sh[1, 1]))
-    both_in(lambda d: sig_copy(2, d).wait_recv())
-    di[0] = fh[0]
-    di[5] = fh[1]
-
-    @pl.loop(0, PC)
-    def _(p):
-        e = [probe(p, k - 2) * di[k] for k in range(6)]
-        y = [apply(k, e[k + 1], e[k], e[k + 2]) for k in range(4)]
-        for k in range(4):
-            gd[p, k] = e[k + 1]
-            gw[p, k] = y[k]
-        z0, z1 = apply(1, y[1], y[0], y[2]), apply(2, y[2], y[1], y[3])
-        g0, g1 = probe(p, 0), probe(p, 1)
-        u0, u1 = dg[0] * y[1], dg[1] * y[2]
-        record(p, (
-            (GG, total(g0 * e[2] + g1 * e[3])),
-            (GG + 1, total(g0 * y[1] + g1 * y[2])),
-            (GG + 2, total(u0 * y[1] + u1 * y[2])),
-            (GG + 3, total(u0 * z0 + u1 * z1)),
-        ))
+    send_sig(1)
+    send_sig(2)
 
     for s in range(2):
         @pl.loop(0, PC)
@@ -382,9 +398,34 @@
             if s == 0:
                 record(p, ((F_MU, mu), (F_NU, nu), (F_W, gy)))
             else:
-                cross = total(u0 * gw[p, 1] + u1 * gw[p, 2])
-                record(p, ((YY + 1, mu), (YY + 2, nu), (GY + 1, gy), (GY + 2, cross)))
+                record(p, ((YY + 1, mu), (YY + 2, nu), (GY + 1, gy)))
             pass_on(1, s, p)
+
+    pass_sig(1)
+    pass_sig(2)
+    both_in(lambda d: sig_copy(1, d).wait_recv())
+    couple(0, sh[0, 1], 0.5 * (sh[0, 0] + sh[0, 1]), 0.5 * (cond[0] + sh[0, 1]) * lo_open)
+    couple(3, sh[1, 0], 0.5 * (cond[1] + sh[1, 0]) * hi_open, 0.5 * (sh[1, 0] + sh[1, 1]))
+    both_in(lambda d: sig_copy(2, d).wait_recv())
+    di[0] = fh[0]
+    di[5] = fh[1]
+
+    @pl.loop(0, PC)
+    def _(p):
+        e = [probe(p, k - 2) * di[k] for k in range(6)]
+        y = [apply(k, e[k + 1], e[k], e[k + 2]) for k in range(4)]
+        for k in range(4):
+            gd[p, k] = e[k + 1]
+            gw[p, k] = y[k]
+        z0, z1 = apply(1, y[1], y[0], y[2]), apply(2, y[2], y[1], y[3])
+        g0, g1 = probe(p, 0), probe(p, 1)
+        u0, u1 = dg[0] * y[1], dg[1] * y[2]
+        record(p, (
+            (GG, total(g0 * e[2] + g1 * e[3])),
+            (GG + 1, total(g0 * y[1] + g1 * y[2])),
+            (GG + 2, total(u0 * y[1] + u1 * y[2])),
+            (GG + 3, total(u0 * z0 + u1 * z1)),
+        ))
 
     for s in range(2):
         @pl.loop(0, PC)
@@ -398,8 +439,9 @@
             if s == 0:
                 record(p, ((F_XI, xi),))
             else:
-                cross = total(u0 * gw[p, 1] + u1 * gw[p, 2])
-                record(p, ((YY + 3, xi), (GY + 3, cross)))
+                k0, k1 = gw[p, 1], gw[p, 2]
+                near = total(dg[0] * a * k0 + dg[1] * b * k1)
+                record(p, ((YY + 3, xi), (GY + 2, near), (GY + 3, total(u0 * k0 + u1 * k1))))
 
     def sum_copy(stage, k, slot):
         return pltpu.make_async_remote_copy(
@@ -530,6 +572,10 @@
 
     for kind in range(3):
         both(lambda d: sig_copy(kind, d).wait_send())
+        for d in range(2):
+            @pl.when(crossing[d][3] & (v == crossing[d][2]))
+            def _():
+                sig_out(kind, d).wait_send()
 
     @pl.loop(0, PC)
     def _(p):
@@ -581,6 +627,7 @@
                 pltpu.VMEM((PC, 4, N, N), f32),
                 pltpu.VMEM((PC, 4, N, N), f32),
                 pltpu.VMEM((3, 2 * PC, N, N), f32),
+                pltpu.VMEM((3, N, N), f32),
                 pltpu.VMEM((6, 4, N, N), f32),
                 pltpu.VMEM((2, N, N), f32),
                 pltpu.VMEM((6, N, N), f32),
@@ -596,6 +643,8 @@
                 dma((3,)),
                 dma((3, 2)),
                 dma((3, 2)),
+                dma((3,)),
+                dma((3,)),
                 dma((3, 2, 2, PC)),
                 dma((3, 2, 2, PC)),
                 dma((3, 2 * PC)),

time: 87.4 us -> 82.7 us (0.946)
  Pallas kernels: 84.5 us -> 79.7 us
    pallas_call x1, Pallas kernels: 84.5 us -> 79.7 us  [per_device(): pl.pallas_call(functools.partial(kernel, npat, layers, group, strength),...]
where the time goes in v4:
time: 82.7 us; the launch traced here: 82.5 us
  Pallas kernels  79.7 us (96%)
  local copies, waits for them, and re-layouts  2.08 us (3%)
    pallas_call x1, Pallas kernels, per_device(): pl.pallas_call(functools.partial(kernel, npat, layers, group, strength),...  79.7 us
    unnamed x4, local copies, waits for them, and re-layouts  2.08 us

profile of v4, /device:TPU:8, one launch (start us, length us, event | category | flops | bytes accessed | tf_op | source)
XLA Modules:
  0.0 82.5 jit_solution(14130232944232398900)
XLA Ops:
  0.6 79.7 %ert_gradient.1 = (f32[2,128,128]{2,1,0:T(8,128)}, f32[1,8]{1,0:T(1,128)}) custom-call(f32[2,128,128]{2,1,0:T(8,128)} %cond_in.1, f32[2,8,128,128]{3,2,1,0:T(8,128)} %wf_in.1, f32[2,8,128,128]{3,2,1,0:T(8,128)} %wa_in.1, s32[128]{0:T(128)} %elec.1, s32[4,8]{1,0:T(4,128)} %bitcast.2, f32[8]{0:T(128)} %obs.1), custom_call_target="tpu_custom_call" | custom-call | tf_op jit(solution)/shard_map/ert_gradient/pallas_call | solution.py:609
  80.4 0.0 copy-start
  80.4 1.6 %copy.10 = f32[2,128,128]{2,1,0:T(8,128)} copy(f32[2,128,128]{2,1,0:T(8,128)} %get-tuple-element.8) | data formatting | bytes 262144
  81.9 0.0 copy-done
  81.9 0.5 copy.11
Async XLA Ops:
  80.4 1.6 %copy-start = (f32[1,8]{1,0:T(1,128)S(1)}, f32[1,8]{1,0:T(1,128)}, u32[]{:S(2)}) copy-start(f32[1,8]{1,0:T(1,128)} %get-tuple-element.5) | copy-start | bytes 100

commit v5 on v4

--- a/solution.py
+++ b/solution.py
@@ -71,6 +71,7 @@
     dg,
     di,
     acc,
+    top,
     tile,
     red,
     kc,
@@ -412,6 +413,7 @@
 
     @pl.loop(0, PC)
     def _(p):
+        pass_on(2, 0, p)
         e = [probe(p, k - 2) * di[k] for k in range(6)]
         y = [apply(k, e[k + 1], e[k], e[k + 2]) for k in range(4)]
         for k in range(4):
@@ -430,7 +432,8 @@
     for s in range(2):
         @pl.loop(0, PC)
         def _(p):
-            pass_on(2, s, p)
+            if s == 0:
+                pass_on(2, 1, p)
             await_halo(2, s, p)
             a, b = w0[s, p, 0], w0[s, p, 1]
             u0 = dg[0] * apply(1, a, wh[s, 0, p], b)
@@ -489,30 +492,39 @@
     wide = jnp.where(trow == tcol, predicted, 0.0)
     pred_out[...] = jnp.sum(wide, axis=0, keepdims=True)[:, :PC]
 
-    @pl.loop(0, PC)
-    def _(p):
-        m = [kc[k, pl.ds(p, 1), :] for k in range(6)]
-
-        def field(s, k):
-            if k in (0, 3):
-                x, d, w = (h[s, k // 3, p] for h in (xh, dh, wh))
-            else:
-                x, d, w = warm[s, k - 1, p], d0[s, p, k - 1], w0[s, p, k - 1]
-            out = x + m[2 * s] * d + m[2 * s + 1] * w
-            if s == 1:
-                out = out + m[4] * gd[p, k] + m[5] * gw[p, k]
-            return out
-
-        f = [field(0, k) for k in range(4)]
-        a = [field(1, k) for k in range(4)]
-        for k in range(3):
-            acc[k] += (f[k + 1] - f[k]) * (a[k + 1] - a[k])
-        for k in range(2):
-            x, y = f[k + 1], a[k + 1]
-            acc[3 + k] += (up_row(x) - x) * (up_row(y) - y)
-            acc[5 + k] += (up_col(x) - x) * (up_col(y) - y)
-
-    for plane in range(2):
+    is_outer = (q == 0) | (q == npat - 1) if npat > 2 else q < 0
+    is_inner = jnp.logical_not(is_outer)
+    outward = jnp.where(q < middle, q - 1, q + 1)
+    inward = jnp.where(q < middle, q + 1, q - 1)
+    height = N // (PIECES // 2)
+
+    def line_copy(leg, j):
+        at = (j // (PIECES // 2), pl.ds(j % (PIECES // 2) * height, height))
+        src = (gb, half, grad)[leg].at[at]
+        dst = (lb[0], lb[1], grad)[leg].at[at]
+        return pltpu.make_async_remote_copy(
+            src, dst, ls.at[leg, j], lr.at[leg, j],
+            device_id=(outward if leg == 2 else inward, v), device_id_type=MESH,
+        )
+
+    def piece(j):
+        return j // (PIECES // 2), slice(j % (PIECES // 2) * height, (j % (PIECES // 2) + 1) * height)
+
+    def field(p, s, k):
+        if k in (0, 3):
+            x, d, w = (h[s, k // 3, p] for h in (xh, dh, wh))
+        else:
+            x, d, w = warm[s, k - 1, p], d0[s, p, k - 1], w0[s, p, k - 1]
+        out = x + kc[2 * s, pl.ds(p, 1), :] * d + kc[2 * s + 1, pl.ds(p, 1), :] * w
+        if s == 1:
+            out = out + kc[4, pl.ds(p, 1), :] * gd[p, k] + kc[5, pl.ds(p, 1), :] * gw[p, k]
+        return out
+
+    def within(plane, x, y):
+        acc[3 + plane] += (up_row(x) - x) * (up_row(y) - y)
+        acc[5 + plane] += (up_col(x) - x) * (up_col(y) - y)
+
+    def finish(plane):
         lo, hi = acc[plane], acc[plane + 1]
         lo = lo * lo_open if plane == 0 else lo
         hi = hi * hi_open if plane == 1 else hi
@@ -520,28 +532,33 @@
         py = jnp.where(cols < N - 1, acc[5 + plane], 0.0)
         gb[plane] = -0.5 * ((lo + hi) + (px + down_row(px)) + (py + down_col(py)))
 
-    is_outer = (q == 0) | (q == npat - 1) if npat > 2 else q < 0
-    is_inner = jnp.logical_not(is_outer)
-    outward = jnp.where(q < middle, q - 1, q + 1)
-    inward = jnp.where(q < middle, q + 1, q - 1)
-    height = N // (PIECES // 2)
-
-    def line_copy(leg, j):
-        at = (j // (PIECES // 2), pl.ds(j % (PIECES // 2) * height, height))
-        src = (gb, half, grad)[leg].at[at]
-        dst = (lb[0], lb[1], grad)[leg].at[at]
-        return pltpu.make_async_remote_copy(
-            src, dst, ls.at[leg, j], lr.at[leg, j],
-            device_id=(outward if leg == 2 else inward, v), device_id_type=MESH,
-        )
-
-    def piece(j):
-        return j // (PIECES // 2), slice(j % (PIECES // 2) * height, (j % (PIECES // 2) + 1) * height)
+        @pl.when(is_outer)
+        def _():
+            for j in range(plane * PIECES // 2, (plane + 1) * PIECES // 2):
+                line_copy(0, j).start()
+
+    @pl.loop(0, PC)
+    def _(p):
+        f = [field(p, 0, k) for k in range(3)]
+        a = [field(p, 1, k) for k in range(3)]
+        top[0, p] = f[2]
+        top[1, p] = a[2]
+        for k in range(2):
+            acc[k] += (f[k + 1] - f[k]) * (a[k + 1] - a[k])
+        within(0, f[1], a[1])
+
+    finish(0)
+
+    @pl.loop(0, PC)
+    def _(p):
+        x, y = top[0, p], top[1, p]
+        acc[2] += (field(p, 0, 3) - x) * (field(p, 1, 3) - y)
+        within(1, x, y)
+
+    finish(1)
 
     @pl.when(is_outer)
     def _():
-        for j in range(PIECES):
-            line_copy(0, j).start()
         for j in range(PIECES):
             line_copy(2, j).wait_recv()
         for j in range(PIECES):
@@ -632,6 +649,7 @@
                 pltpu.VMEM((2, N, N), f32),
                 pltpu.VMEM((6, N, N), f32),
                 pltpu.VMEM((7, N, N), f32),
+                pltpu.VMEM((2, PC, N, N), f32),
                 pltpu.VMEM((PC, N), f32),
                 pltpu.VMEM((2, widest, PC, N), f32),
                 pltpu.VMEM((6, PC, N), f32),
@@ -655,7 +673,7 @@
                 dma((3, PIECES)),
             ],
             compiler_params=pltpu.CompilerParams(
-                collective_id=0, has_side_effects=True, vmem_limit_bytes=58 * 2**20
+                collective_id=0, has_side_effects=True, vmem_limit_bytes=int(53.7 * 2**20)
             ),
             name="ert_gradient",
         )(conductivity, warm_forward, warm_adjoint, electrodes, patterns.T, observed)

time: 82.7 us -> 78.9 us (0.954)
  Pallas kernels: 79.7 us -> 75.5 us
    pallas_call x1, Pallas kernels: 79.7 us -> 75.5 us  [per_device(): pl.pallas_call(functools.partial(kernel, npat, layers, group, strength),...]
    unnamed x4 -> x8, local copies, waits for them, and re-layouts: 2.08 us -> 2.51 us
where the time goes in v5:
time: 78.9 us; the launch traced here: 78.7 us
  Pallas kernels  75.5 us (96%)
  local copies, waits for them, and re-layouts  2.51 us (3%)
    pallas_call x1, Pallas kernels, per_device(): pl.pallas_call(functools.partial(kernel, npat, layers, group, strength),...  75.5 us
    unnamed x8, local copies, waits for them, and re-layouts  2.51 us

profile of v5, /device:TPU:8, one launch (start us, length us, event | category | flops | bytes accessed | tf_op | source)
XLA Modules:
  0.0 78.7 jit_solution(9156056503006269545)
XLA Ops:
  0.6 0.0 copy-start.2
  0.6 0.0 copy-start.1
  0.7 0.6 copy-done.2
  1.3 0.0 copy-done.1
  1.3 0.0 copy-start
  1.3 0.7 copy-done
  2.0 75.5 %ert_gradient.1 = (f32[2,128,128]{2,1,0:T(8,128)S(1)}, f32[1,8]{1,0:T(1,128)S(1)}) custom-call(f32[2,128,128]{2,1,0:T(8,128)} %cond_in.1, f32[2,8,128,128]{3,2,1,0:T(8,128)} %wf_in.1, f32[2,8,128,128]{3,2,1,0:T(8,128)} %wa_in.1, s32[128]{0:T(128)S(1)} %copy-done.1, s32[4,8]{1,0:T(4,128)S(1)} %bitcast.2, f32[8]{0:T(128)S(1)} %copy-done.2), custom_call_target="tpu_custom_call" | custom-call | tf_op jit(solution)/shard_map/ert_gradient/pallas_call | solution.py:626
  77.5 0.7 copy.10
  78.2 0.5 copy.11
Async XLA Ops:
  0.6 0.7 copy-start.2
  0.6 0.7 copy-start.1
  1.3 0.7 copy-start

commit v6 on v5

--- a/solution.py
+++ b/solution.py
@@ -49,13 +49,16 @@
     cond_in,
     wf_in,
     wa_in,
-    elec,
-    pats,
-    obs,
+    elec_in,
+    pats_in,
+    obs_in,
     grad_out,
     pred_out,
     cond,
     warm,
+    elec,
+    pats,
+    obs,
     sh,
     fh,
     xh,
@@ -116,6 +119,9 @@
         pltpu.make_async_copy(cond_in, cond, in_s.at[0]),
         pltpu.make_async_copy(wf_in, warm.at[0], in_s.at[1]),
         pltpu.make_async_copy(wa_in, warm.at[1], in_s.at[2]),
+        pltpu.make_async_copy(elec_in, elec, in_s.at[3]),
+        pltpu.make_async_copy(pats_in, pats, in_s.at[4]),
+        pltpu.make_async_copy(obs_in, obs, in_s.at[5]),
     ]
 
     def member(stage, k):
@@ -453,12 +459,32 @@
             device_id=(q, member(stage, k)), device_id_type=MESH,
         )
 
+    def halos_have_left():
+        for kind in range(3):
+            both(lambda d: sig_copy(kind, d).wait_send())
+            for d in range(2):
+                @pl.when(crossing[d][3] & (v == crossing[d][2]))
+                def _():
+                    sig_out(kind, d).wait_send()
+
+        @pl.loop(0, PC)
+        def _(p):
+            for stage in range(3):
+                for s in range(2):
+                    both(lambda d: halo_copy(stage, s, d, p).wait_send())
+                    for d in range(2):
+                        @pl.when(crossing[d][3] & (v == crossing[d][2]))
+                        def _():
+                            detour_out(stage, s, d, p).wait_send()
+
     value = tile[...]
     for stage in range(2):
         mine, size = rank[stage], sizes[stage]
         red[stage, mine] = value
         for j in range(1, size):
             sum_copy(stage, lax.rem(mine + j, size), mine).start()
+        if stage == 1:
+            halos_have_left()
         for j in range(1, size):
             k = lax.rem(mine + j, size)
             sum_copy(stage, k, k).wait_recv()
@@ -587,23 +613,6 @@
 
     grad_out[...] = grad[...]
 
-    for kind in range(3):
-        both(lambda d: sig_copy(kind, d).wait_send())
-        for d in range(2):
-            @pl.when(crossing[d][3] & (v == crossing[d][2]))
-            def _():
-                sig_out(kind, d).wait_send()
-
-    @pl.loop(0, PC)
-    def _(p):
-        for stage in range(3):
-            for s in range(2):
-                both(lambda d: halo_copy(stage, s, d, p).wait_send())
-                for d in range(2):
-                    @pl.when(crossing[d][3] & (v == crossing[d][2]))
-                    def _():
-                        detour_out(stage, s, d, p).wait_send()
-
     for stage in range(2):
         for j in range(1, sizes[stage]):
             sum_copy(stage, lax.rem(rank[stage] + j, sizes[stage]), rank[stage]).wait_send()
@@ -617,7 +626,6 @@
         planes = conductivity.shape[0]
         strength = 2.0 * math.sqrt(layers * planes * PLANE)
         vmem = pl.BlockSpec(memory_space=pltpu.VMEM)
-        smem = pl.BlockSpec(memory_space=pltpu.SMEM)
         hbm = pl.BlockSpec(memory_space=pltpu.HBM)
         f32 = jnp.float32
         dma = pltpu.SemaphoreType.DMA
@@ -629,11 +637,14 @@
                 jax.ShapeDtypeStruct((2, N, N), f32),
                 jax.ShapeDtypeStruct((1, PC), f32),
             ),
-            in_specs=[hbm, hbm, hbm, smem, smem, smem],
+            in_specs=[hbm] * 6,
             out_specs=(vmem, vmem),
             scratch_shapes=[
                 pltpu.VMEM((2, N, N), f32),
                 pltpu.VMEM((2, 2, PC, N, N), f32),
+                pltpu.SMEM(electrodes.shape, jnp.int32),
+                pltpu.SMEM((4, PC), jnp.int32),
+                pltpu.SMEM((PC,), f32),
                 pltpu.VMEM((2, 2, N, N), f32),
                 pltpu.VMEM((2, N, N), f32),
                 pltpu.VMEM((2, 2, PC, N, N), f32),
@@ -658,7 +669,7 @@
                 pltpu.VMEM((2, N, N), f32),
                 pltpu.VMEM((2, N, N), f32),
                 pltpu.VMEM((2, N, N), f32),
-                dma((3,)),
+                dma((6,)),
                 dma((3, 2)),
                 dma((3, 2)),
                 dma((3,)),
@@ -673,10 +684,13 @@
                 dma((3, PIECES)),
             ],
             compiler_params=pltpu.CompilerParams(
-                collective_id=0, has_side_effects=True, vmem_limit_bytes=int(53.7 * 2**20)
+                collective_id=0, has_side_effects=True, vmem_limit_bytes=48 * 2**20
             ),
             name="ert_gradient",
-        )(conductivity, warm_forward, warm_adjoint, electrodes, patterns.T, observed)
+        )(*(
+            pltpu.with_memory_space_constraint(x, pltpu.HBM)
+            for x in (conductivity, warm_forward, warm_adjoint, electrodes, patterns.T, observed)
+        ))
         return gradient, predicted.reshape(PC)
 
     in_specs = (

time: 78.9 us -> 76.8 us (0.973)
  local copies, waits for them, and re-layouts: 2.51 us -> 1.17 us
    unnamed x8 -> x2, local copies, waits for them, and re-layouts: 2.51 us -> 1.17 us
where the time goes in v6:
time: 76.8 us; the launch traced here: 76.7 us
  Pallas kernels  74.8 us (97%)
  local copies, waits for them, and re-layouts  1.17 us (2%)
    pallas_call x1, Pallas kernels, per_device(): pl.pallas_call(functools.partial(kernel, npat, layers, group, strength),...  74.8 us

profile of v6, /device:TPU:8, one launch (start us, length us, event | category | flops | bytes accessed | tf_op | source)
XLA Modules:
  0.0 76.7 jit_solution(1848658649143798442)
XLA Ops:
  0.6 74.8 %ert_gradient.1 = (f32[2,128,128]{2,1,0:T(8,128)S(1)}, f32[1,8]{1,0:T(1,128)S(1)}) custom-call(f32[2,128,128]{2,1,0:T(8,128)} %cond_in.1, f32[2,8,128,128]{3,2,1,0:T(8,128)} %wf_in.1, f32[2,8,128,128]{3,2,1,0:T(8,128)} %wa_in.1, s32[128]{0:T(128)} %elec_in.1, s32[4,8]{1,0:T(4,128)} %bitcast.3, f32[8]{0:T(128)} %obs_in.1), custom_call_target="tpu_custom_call" | custom-call | tf_op jit(solution)/shard_map/ert_gradient/pallas_call | solution.py:634
  75.5 0.7 copy.10
  76.1 0.5 copy.11

commit v7 on v6

--- a/solution.py
+++ b/solution.py
@@ -114,6 +114,8 @@
         (lower, upper, 0, inner),
         (upper, lower, last, jnp.logical_not(inner)),
     )
+    aside = jnp.where(inner, 6, 24) if layers == 64 else 0
+    beside = (aside, upper + aside if layers == 64 else last)
 
     local = [
         pltpu.make_async_copy(cond_in, cond, in_s.at[0]),
@@ -156,6 +158,21 @@
         expected = expected + on_path.astype(jnp.int32)
         expected = expected + 2 * (taken & (v == via)).astype(jnp.int32)
 
+    for d in range(2):
+        source, target = crossing[d][:2]
+        at_end, at_via = (v == source) | (v == target), v == beside[d]
+
+        @pl.when(at_end)
+        def _():
+            greet((q, beside[d]))
+
+        @pl.when(at_via)
+        def _():
+            greet((q, source))
+            greet((q, target))
+
+        expected = expected + at_end.astype(jnp.int32) + 2 * at_via.astype(jnp.int32)
+
     for stage in range(2):
         for j in range(1, sizes[stage]):
             greet((q, member(stage, lax.rem(rank[stage] + j, sizes[stage]))))
@@ -213,10 +230,16 @@
             device_id=neighbour(d), device_id_type=MESH,
         )
 
+    def sig_via(kind, d):
+        return beside[d] if kind else crossing[d][2]
+
+    def sig_detour(kind, d, at):
+        return v == at if kind else crossing[d][3] & (v == at)
+
     def sig_in(kind, d):
         return pltpu.make_async_remote_copy(
             sig_ends(kind, d)[0], sb.at[kind], sig_s.at[kind, d], sig_rr.at[kind],
-            device_id=(q, crossing[d][2]), device_id_type=MESH,
+            device_id=(q, sig_via(kind, d)), device_id_type=MESH,
         )
 
     def sig_out(kind, d):
@@ -273,7 +296,7 @@
 
     def send_sig(kind):
         for d in range(2):
-            around = crossing[d][3] & (v == crossing[d][0])
+            around = sig_detour(kind, d, crossing[d][0])
 
             @pl.when(exists[d] & jnp.logical_not(around))
             def _():
@@ -285,7 +308,7 @@
 
     def pass_sig(kind):
         for d in range(2):
-            @pl.when(crossing[d][3] & (v == crossing[d][2]))
+            @pl.when(sig_detour(kind, d, sig_via(kind, d)))
             def _():
                 sig_in(kind, d).wait_recv()
                 sig_out(kind, d).start()
@@ -342,6 +365,8 @@
     both_in(lambda d: sig_copy(0, d).wait_recv())
     couple(1, cond[0], 0.5 * (cond[0] + sh[0, 1]) * lo_open, 0.5 * (cond[0] + cond[1]))
     couple(2, cond[1], 0.5 * (cond[0] + cond[1]), 0.5 * (cond[1] + sh[1, 0]) * hi_open)
+    send_sig(1)
+    send_sig(2)
 
     def apply(k, x, below, above):
         y = co[ZL, k] * below + co[ZH, k] * above
@@ -385,8 +410,32 @@
                 record(p, ((YY, rho), (GY, ge)))
             pass_on(0, s, p)
 
-    send_sig(1)
-    send_sig(2)
+    pass_sig(1)
+    pass_sig(2)
+    both_in(lambda d: sig_copy(1, d).wait_recv())
+    couple(0, sh[0, 1], 0.5 * (sh[0, 0] + sh[0, 1]), 0.5 * (cond[0] + sh[0, 1]) * lo_open)
+    couple(3, sh[1, 0], 0.5 * (cond[1] + sh[1, 0]) * hi_open, 0.5 * (sh[1, 0] + sh[1, 1]))
+    both_in(lambda d: sig_copy(2, d).wait_recv())
+    di[0] = fh[0]
+    di[5] = fh[1]
+
+    @pl.loop(0, PC)
+    def _(p):
+        pass_on(1, 0, p)
+        e = [probe(p, k - 2) * di[k] for k in range(6)]
+        y = [apply(k, e[k + 1], e[k], e[k + 2]) for k in range(4)]
+        for k in range(4):
+            gd[p, k] = e[k + 1]
+            gw[p, k] = y[k]
+        z0, z1 = apply(1, y[1], y[0], y[2]), apply(2, y[2], y[1], y[3])
+        g0, g1 = probe(p, 0), probe(p, 1)
+        u0, u1 = dg[0] * y[1], dg[1] * y[2]
+        record(p, (
+            (GG, total(g0 * e[2] + g1 * e[3])),
+            (GG + 1, total(g0 * y[1] + g1 * y[2])),
+            (GG + 2, total(u0 * y[1] + u1 * y[2])),
+            (GG + 3, total(u0 * z0 + u1 * z1)),
+        ))
 
     for s in range(2):
         @pl.loop(0, PC)
@@ -406,34 +455,7 @@
                 record(p, ((F_MU, mu), (F_NU, nu), (F_W, gy)))
             else:
                 record(p, ((YY + 1, mu), (YY + 2, nu), (GY + 1, gy)))
-            pass_on(1, s, p)
-
-    pass_sig(1)
-    pass_sig(2)
-    both_in(lambda d: sig_copy(1, d).wait_recv())
-    couple(0, sh[0, 1], 0.5 * (sh[0, 0] + sh[0, 1]), 0.5 * (cond[0] + sh[0, 1]) * lo_open)
-    couple(3, sh[1, 0], 0.5 * (cond[1] + sh[1, 0]) * hi_open, 0.5 * (sh[1, 0] + sh[1, 1]))
-    both_in(lambda d: sig_copy(2, d).wait_recv())
-    di[0] = fh[0]
-    di[5] = fh[1]
-
-    @pl.loop(0, PC)
-    def _(p):
-        pass_on(2, 0, p)
-        e = [probe(p, k - 2) * di[k] for k in range(6)]
-        y = [apply(k, e[k + 1], e[k], e[k + 2]) for k in range(4)]
-        for k in range(4):
-            gd[p, k] = e[k + 1]
-            gw[p, k] = y[k]
-        z0, z1 = apply(1, y[1], y[0], y[2]), apply(2, y[2], y[1], y[3])
-        g0, g1 = probe(p, 0), probe(p, 1)
-        u0, u1 = dg[0] * y[1], dg[1] * y[2]
-        record(p, (
-            (GG, total(g0 * e[2] + g1 * e[3])),
-            (GG + 1, total(g0 * y[1] + g1 * y[2])),
-            (GG + 2, total(u0 * y[1] + u1 * y[2])),
-            (GG + 3, total(u0 * z0 + u1 * z1)),
-        ))
+            pass_on(1 + s, 1 - s, p)
 
     for s in range(2):
         @pl.loop(0, PC)
@@ -463,7 +485,7 @@
         for kind in range(3):
             both(lambda d: sig_copy(kind, d).wait_send())
             for d in range(2):
-                @pl.when(crossing[d][3] & (v == crossing[d][2]))
+                @pl.when(sig_detour(kind, d, sig_via(kind, d)))
                 def _():
                     sig_out(kind, d).wait_send()
 

time: 76.8 us -> 103 us (1.34)
  Pallas kernels: 74.8 us -> 101 us
    pallas_call x1, Pallas kernels: 74.8 us -> 101 us  [per_device(): pl.pallas_call(functools.partial(kernel, npat, layers, group, strength),...]
where the time goes in v7:
time: 103 us
  Pallas kernels  101 us (98%)
  local copies, waits for them, and re-layouts  1.17 us (1%)
    pallas_call x1, Pallas kernels, per_device(): pl.pallas_call(functools.partial(kernel, npat, layers, group, strength),...  101 us

profile of v7, /device:TPU:8, one launch (start us, length us, event | category | flops | bytes accessed | tf_op | source)
XLA Modules:
  0.0 102.5 jit_solution(14517877285246057090)
XLA Ops:
  0.6 100.7 %ert_gradient.1 = (f32[2,128,128]{2,1,0:T(8,128)S(1)}, f32[1,8]{1,0:T(1,128)S(1)}) custom-call(f32[2,128,128]{2,1,0:T(8,128)} %cond_in.1, f32[2,8,128,128]{3,2,1,0:T(8,128)} %wf_in.1, f32[2,8,128,128]{3,2,1,0:T(8,128)} %wa_in.1, s32[128]{0:T(128)} %elec_in.1, s32[4,8]{1,0:T(4,128)} %bitcast.3, f32[8]{0:T(128)} %obs_in.1), custom_call_target="tpu_custom_call" | custom-call | tf_op jit(solution)/shard_map/ert_gradient/pallas_call | solution.py:656
  101.4 0.7 copy.10
  102.0 0.5 copy.11

commit v8 on v7

--- a/solution.py
+++ b/solution.py
@@ -114,8 +114,6 @@
         (lower, upper, 0, inner),
         (upper, lower, last, jnp.logical_not(inner)),
     )
-    aside = jnp.where(inner, 6, 24) if layers == 64 else 0
-    beside = (aside, upper + aside if layers == 64 else last)
 
     local = [
         pltpu.make_async_copy(cond_in, cond, in_s.at[0]),
@@ -158,21 +156,6 @@
         expected = expected + on_path.astype(jnp.int32)
         expected = expected + 2 * (taken & (v == via)).astype(jnp.int32)
 
-    for d in range(2):
-        source, target = crossing[d][:2]
-        at_end, at_via = (v == source) | (v == target), v == beside[d]
-
-        @pl.when(at_end)
-        def _():
-            greet((q, beside[d]))
-
-        @pl.when(at_via)
-        def _():
-            greet((q, source))
-            greet((q, target))
-
-        expected = expected + at_end.astype(jnp.int32) + 2 * at_via.astype(jnp.int32)
-
     for stage in range(2):
         for j in range(1, sizes[stage]):
             greet((q, member(stage, lax.rem(rank[stage] + j, sizes[stage]))))
@@ -230,16 +213,10 @@
             device_id=neighbour(d), device_id_type=MESH,
         )
 
-    def sig_via(kind, d):
-        return beside[d] if kind else crossing[d][2]
-
-    def sig_detour(kind, d, at):
-        return v == at if kind else crossing[d][3] & (v == at)
-
     def sig_in(kind, d):
         return pltpu.make_async_remote_copy(
             sig_ends(kind, d)[0], sb.at[kind], sig_s.at[kind, d], sig_rr.at[kind],
-            device_id=(q, sig_via(kind, d)), device_id_type=MESH,
+            device_id=(q, crossing[d][2]), device_id_type=MESH,
         )
 
     def sig_out(kind, d):
@@ -296,7 +273,7 @@
 
     def send_sig(kind):
         for d in range(2):
-            around = sig_detour(kind, d, crossing[d][0])
+            around = crossing[d][3] & (v == crossing[d][0])
 
             @pl.when(exists[d] & jnp.logical_not(around))
             def _():
@@ -308,7 +285,7 @@
 
     def pass_sig(kind):
         for d in range(2):
-            @pl.when(sig_detour(kind, d, sig_via(kind, d)))
+            @pl.when(crossing[d][3] & (v == crossing[d][2]))
             def _():
                 sig_in(kind, d).wait_recv()
                 sig_out(kind, d).start()
@@ -485,7 +462,7 @@
         for kind in range(3):
             both(lambda d: sig_copy(kind, d).wait_send())
             for d in range(2):
-                @pl.when(sig_detour(kind, d, sig_via(kind, d)))
+                @pl.when(crossing[d][3] & (v == crossing[d][2]))
                 def _():
                     sig_out(kind, d).wait_send()
 

time: 103 us -> 76.9 us (0.75)
  Pallas kernels: 101 us -> 75 us
    pallas_call x1, Pallas kernels: 101 us -> 75 us  [per_device(): pl.pallas_call(functools.partial(kernel, npat, layers, group, strength),...]
where the time goes in v8:
time: 76.9 us; the launch traced here: 76.8 us
  Pallas kernels  75 us (98%)
  local copies, waits for them, and re-layouts  1.17 us (2%)
    pallas_call x1, Pallas kernels, per_device(): pl.pallas_call(functools.partial(kernel, npat, layers, group, strength),...  75 us

profile of v8, /device:TPU:8, one launch (start us, length us, event | category | flops | bytes accessed | tf_op | source)
XLA Modules:
  0.0 76.8 jit_solution(5484539946655061614)
XLA Ops:
  0.6 75.0 %ert_gradient.1 = (f32[2,128,128]{2,1,0:T(8,128)S(1)}, f32[1,8]{1,0:T(1,128)S(1)}) custom-call(f32[2,128,128]{2,1,0:T(8,128)} %cond_in.1, f32[2,8,128,128]{3,2,1,0:T(8,128)} %wf_in.1, f32[2,8,128,128]{3,2,1,0:T(8,128)} %wa_in.1, s32[128]{0:T(128)} %elec_in.1, s32[4,8]{1,0:T(4,128)} %bitcast.3, f32[8]{0:T(128)} %obs_in.1), custom_call_target="tpu_custom_call" | custom-call | tf_op jit(solution)/shard_map/ert_gradient/pallas_call | solution.py:633
  75.6 0.7 copy.10
  76.2 0.5 copy.11

commit v9 on v8

--- a/solution.py
+++ b/solution.py
@@ -39,6 +39,10 @@
 def total(x):
     part = jnp.sum(x.reshape(N // 8, 8, N), axis=0)
     return jnp.sum(jnp.sum(part, axis=1, keepdims=True), axis=0, keepdims=True)
+
+
+def far_first(size):
+    return sorted(range(1, size), key=lambda j: abs(j - size // 2))
 
 
 def kernel(
@@ -156,8 +160,8 @@
         expected = expected + on_path.astype(jnp.int32)
         expected = expected + 2 * (taken & (v == via)).astype(jnp.int32)
 
-    for stage in range(2):
-        for j in range(1, sizes[stage]):
+    for stage in (1, 0):
+        for j in far_first(sizes[stage]):
             greet((q, member(stage, lax.rem(rank[stage] + j, sizes[stage]))))
     below, above = q > 0, q < npat - 1
 
@@ -431,7 +435,8 @@
             if s == 0:
                 record(p, ((F_MU, mu), (F_NU, nu), (F_W, gy)))
             else:
-                record(p, ((YY + 1, mu), (YY + 2, nu), (GY + 1, gy)))
+                cross = total(u0 * gw[p, 1] + u1 * gw[p, 2])
+                record(p, ((YY + 1, mu), (YY + 2, nu), (GY + 1, gy), (GY + 2, cross)))
             pass_on(1 + s, 1 - s, p)
 
     for s in range(2):
@@ -447,9 +452,8 @@
             if s == 0:
                 record(p, ((F_XI, xi),))
             else:
-                k0, k1 = gw[p, 1], gw[p, 2]
-                near = total(dg[0] * a * k0 + dg[1] * b * k1)
-                record(p, ((YY + 3, xi), (GY + 2, near), (GY + 3, total(u0 * k0 + u1 * k1))))
+                cross = total(u0 * gw[p, 1] + u1 * gw[p, 2])
+                record(p, ((YY + 3, xi), (GY + 3, cross)))
 
     def sum_copy(stage, k, slot):
         return pltpu.make_async_remote_copy(
@@ -480,7 +484,7 @@
     for stage in range(2):
         mine, size = rank[stage], sizes[stage]
         red[stage, mine] = value
-        for j in range(1, size):
+        for j in far_first(size):
             sum_copy(stage, lax.rem(mine + j, size), mine).start()
         if stage == 1:
             halos_have_left()

time: 76.9 us -> 76.9 us (level)
  no operation moved by 1% of the time
where the time goes in v9:
time: 76.9 us; the launch traced here: 76.8 us
  Pallas kernels  74.9 us (97%)
  local copies, waits for them, and re-layouts  1.17 us (2%)
    pallas_call x1, Pallas kernels, per_device(): pl.pallas_call(functools.partial(kernel, npat, layers, group, strength),...  74.9 us

profile of v9, /device:TPU:8, one launch (start us, length us, event | category | flops | bytes accessed | tf_op | source)
XLA Modules:
  0.0 76.8 jit_solution(11265520060565214101)
XLA Ops:
  0.6 74.9 %ert_gradient.1 = (f32[2,128,128]{2,1,0:T(8,128)S(1)}, f32[1,8]{1,0:T(1,128)S(1)}) custom-call(f32[2,128,128]{2,1,0:T(8,128)} %cond_in.1, f32[2,8,128,128]{3,2,1,0:T(8,128)} %wf_in.1, f32[2,8,128,128]{3,2,1,0:T(8,128)} %wa_in.1, s32[128]{0:T(128)} %elec_in.1, s32[4,8]{1,0:T(4,128)} %bitcast.3, f32[8]{0:T(128)} %obs_in.1), custom_call_target="tpu_custom_call" | custom-call | tf_op jit(solution)/shard_map/ert_gradient/pallas_call | solution.py:637
  75.6 0.7 copy.10
  76.2 0.5 copy.11

commit v10 on v9

--- a/solution.py
+++ b/solution.py
@@ -13,7 +13,7 @@
 N = 128
 PLANE = N * N
 PC = 8
-PIECES = 8
+PIECES = 4
 
 ZL, ZH, XM, XP, YM, YP = range(6)
 F_RHO, F_MU, F_NU, F_XI, F_X, F_D, F_W = range(7)

time: 76.9 us -> 77 us (level)
  no operation moved by 1% of the time
where the time goes in v10:
time: 77 us; the launch traced here: 76.9 us
  Pallas kernels  75.1 us (98%)
  local copies, waits for them, and re-layouts  1.17 us (2%)
    pallas_call x1, Pallas kernels, per_device(): pl.pallas_call(functools.partial(kernel, npat, layers, group, strength),...  75.1 us

profile of v10, /device:TPU:8, one launch (start us, length us, event | category | flops | bytes accessed | tf_op | source)
XLA Modules:
  0.0 76.9 jit_solution(15404433993914390492)
XLA Ops:
  0.6 75.1 %ert_gradient.1 = (f32[2,128,128]{2,1,0:T(8,128)S(1)}, f32[1,8]{1,0:T(1,128)S(1)}) custom-call(f32[2,128,128]{2,1,0:T(8,128)} %cond_in.1, f32[2,8,128,128]{3,2,1,0:T(8,128)} %wf_in.1, f32[2,8,128,128]{3,2,1,0:T(8,128)} %wa_in.1, s32[128]{0:T(128)} %elec_in.1, s32[4,8]{1,0:T(4,128)} %bitcast.3, f32[8]{0:T(128)} %obs_in.1), custom_call_target="tpu_custom_call" | custom-call | tf_op jit(solution)/shard_map/ert_gradient/pallas_call | solution.py:637
  75.7 0.7 copy.10
  76.4 0.5 copy.11

commit v11 on v8

--- a/solution.py
+++ b/solution.py
@@ -378,6 +378,7 @@
             d0[s, p, 0] = e0
             d0[s, p, 1] = e1
             send_halo(1, s, p)
+            pass_on(0, s, p)
             g0, g1 = probe(p, 0), probe(p, 1)
             rho = total(dg[0] * e0 * e0 + dg[1] * e1 * e1)
             ge = total(g0 * e0 + g1 * e1)
@@ -385,7 +386,6 @@
                 record(p, ((F_RHO, rho), (F_D, ge), (F_X, total(g0 * a + g1 * b))))
             else:
                 record(p, ((YY, rho), (GY, ge)))
-            pass_on(0, s, p)
 
     pass_sig(1)
     pass_sig(2)
@@ -424,6 +424,7 @@
             w0[s, p, 0] = y0
             w0[s, p, 1] = y1
             send_halo(2, s, p)
+            pass_on(1 + s, 1 - s, p)
             u0, u1 = dg[0] * y0, dg[1] * y1
             mu = total(u0 * a + u1 * b)
             nu = total(u0 * y0 + u1 * y1)
@@ -432,7 +433,6 @@
                 record(p, ((F_MU, mu), (F_NU, nu), (F_W, gy)))
             else:
                 record(p, ((YY + 1, mu), (YY + 2, nu), (GY + 1, gy)))
-            pass_on(1 + s, 1 - s, p)
 
     for s in range(2):
         @pl.loop(0, PC)

time: 76.9 us -> 76.9 us (level)
  no operation moved by 1% of the time
where the time goes in v11:
time: 76.9 us; the launch traced here: 76.8 us
  Pallas kernels  75 us (98%)
  local copies, waits for them, and re-layouts  1.17 us (2%)
    pallas_call x1, Pallas kernels, per_device(): pl.pallas_call(functools.partial(kernel, npat, layers, group, strength),...  75 us

profile of v11, /device:TPU:8, one launch (start us, length us, event | category | flops | bytes accessed | tf_op | source)
XLA Modules:
  0.0 76.8 jit_solution(11950159404630376701)
XLA Ops:
  0.6 75.0 %ert_gradient.1 = (f32[2,128,128]{2,1,0:T(8,128)S(1)}, f32[1,8]{1,0:T(1,128)S(1)}) custom-call(f32[2,128,128]{2,1,0:T(8,128)} %cond_in.1, f32[2,8,128,128]{3,2,1,0:T(8,128)} %wf_in.1, f32[2,8,128,128]{3,2,1,0:T(8,128)} %wa_in.1, s32[128]{0:T(128)} %elec_in.1, s32[4,8]{1,0:T(4,128)} %bitcast.3, f32[8]{0:T(128)} %obs_in.1), custom_call_target="tpu_custom_call" | custom-call | tf_op jit(solution)/shard_map/ert_gradient/pallas_call | solution.py:633
  75.6 0.7 copy.10
  76.2 0.5 copy.11
